TPU v7x, 128 devices: a whole 4x4x4 slice. The times are simulated.
128 devices in a mesh: va: 8 (over x, z_hi), vb: 8 (over z_lo, y), pair: 2 (over core).
Axes of the slice: x: 4, y: 4, z: 4 (z_hi: 2, z_lo: 2; z = z_hi * 2 + z_lo), core: 2. Of those that a mesh axis runs over, the one named last changes fastest.
Arguments:
- left_fit: bfloat16 [30, 2048, 1536], P('pair', 'va'), may hold values from -0.5 to 0.5
- right_fit: bfloat16 [30, 2048, 1536], P('pair', 'vb'), may hold values from -0.5 to 0.5
- occ_energy: float32 [8], replicated, may hold values from -1.5 to -0.3
- virt_energy: float32 [2048], replicated, may hold values from 0.2 to 2
- pair_list: int32 [30, 2], P('pair'), may hold values from 0 to 7, as said below
- domain_blocks: int32 [30, 12], P('pair'), may hold values from 0 to 31, as said below
Outputs:
- density: float32 [4096, 8, 2048], P(('vb', 'pair'), None, 'va')
Inputs may be any that keep to these rules, and one draw needn't show every extreme that they name: `domain_blocks`: the 12 entries of a row are distinct. `pair_list`: each row holds two orbitals i <= j, and no two rows are the same pair.
All inputs are finite; a program needn't handle non-finite values.
Results may differ from a plain program's by a relative error of at most 0.0028.
Values may be sent and summed in bfloat16 or wider, within the bound.
No kernel may reach another device: no remote copies, remote signals or barrier semaphores. Data moves between devices by JAX's collectives and lax.ppermute only.
A program may use at most 192 MiB of HBM per device.

v0:
```python
import itertools

import jax
import jax.numpy as jnp
from jax import lax
from jax.experimental import pallas as pl
from jax.experimental.pallas import tpu as pltpu
from jax.sharding import PartitionSpec as P


BLOCK = 128
AUX_BLK = 32
CHUNKS = 5
SPLIT = 4
PER_OWNER = 4
AXES = ("va", "vb", "pair")
DETOURS = (
    (0, 3, 3), (1, 3, 0), (0, 2, 3), (3, 0, 1), (0, 2, 1), (3, 1, 0), (0, 1, 1), (1, 0, 2), (2, 2, 0), (1, 0, 3),
)


def to_flat(x, y, z, core):
    va = x * 2 + z // 2
    vb = (z % 2) * 4 + y
    return (va * 8 + vb) * 2 + core


def mirror_chip(x, y, z):
    va, vb = x * 2 + z // 2, (z % 2) * 4 + y
    va, vb = vb, va
    return va // 2, vb % 4, (va % 2) * 2 + vb // 4


def detour_pairs(piece):
    out, back = [], []
    for x, y, z, core in itertools.product(range(4), range(4), range(4), range(2)):
        dx, dy, dz = DETOURS[core * CHUNKS + piece]
        mid = ((x + dx) % 4, (y + dy) % 4, (z + dz) % 4)
        out.append((to_flat(x, y, z, core), to_flat(*mid, core)))
        back.append((to_flat(*mid, core), to_flat(*mirror_chip(x, y, z), core)))
    return out, back


def coulomb_kernel(start, chunks, left_ref, right_ref, *refs):
    out_refs, (left_buf, right_buf, sems) = refs[-3 - chunks : -3], refs[-3:]
    count = out_refs[0].shape[0]
    copies = []
    for p in range(count * len(out_refs)):
        pair = [
            pltpu.make_async_copy(left_ref.at[start + p], left_buf.at[p], sems.at[0, p]),
            pltpu.make_async_copy(right_ref.at[start + p], right_buf.at[p], sems.at[1, p]),
        ]
        for copy in pair:
            copy.start()
        copies.append(pair)
    for p, pair in enumerate(copies):
        for copy in pair:
            copy.wait()
        out_refs[p // count][p % count] = lax.dot_general(
            left_buf[p], right_buf[p], (((1,), (1,)), ((), ())), preferred_element_type=jnp.float32
        ).astype(jnp.bfloat16)


def coulomb(left_fit, right_fit, start, count, chunks, after=()):
    _, rows, dom = left_fit.shape
    total = count * chunks
    hbm = pl.BlockSpec(memory_space=pl.ANY)
    return pl.pallas_call(
        lambda *refs: coulomb_kernel(start, chunks, *refs),
        in_specs=[hbm] * (2 + len(after)),
        out_specs=[pl.BlockSpec(memory_space=pltpu.VMEM)] * chunks,
        out_shape=[jax.ShapeDtypeStruct((count, rows, rows), jnp.bfloat16)] * chunks,
        scratch_shapes=[
            pltpu.VMEM((total, rows, dom), jnp.bfloat16),
            pltpu.VMEM((total, rows, dom), jnp.bfloat16),
            pltpu.SemaphoreType.DMA((2, total)),
        ],
        cost_estimate=pl.CostEstimate(
            flops=2 * total * rows * rows * dom,
            bytes_accessed=4 * total * rows * dom + 2 * total * rows * rows,
            transcendentals=0,
        ),
        compiler_params=pltpu.CompilerParams(vmem_limit_bytes=60 << 20),
        name="coulomb",
    )(left_fit, right_fit, *after)


def fetch(refs, buf_ref, sems):
    copies = [
        pltpu.make_async_copy(ref, buf_ref.at[n], sems.at[n]) for n, ref in enumerate(refs)
    ]
    for copy in copies:
        copy.start()
    return copies


def amplitude_kernel(chunks, *refs):
    core_ref, occ_ref, pair_ref = refs[:3]
    keep_ref, send_ref, work_ref, buf_ref, sems = refs[-5:]
    refs = refs[:-5]
    ea_ref, eb_ref = refs[-2 - 2 * chunks : -2 * chunks]
    copies = fetch(refs[-2 * chunks :], buf_ref, sems)
    tiles = [buf_ref.at[n] for n in range(chunks)]
    mirrors = [buf_ref.at[chunks + n] for n in range(chunks)]
    half = keep_ref.shape[1]
    count = tiles[0].shape[0]
    core = core_ref[0]
    base = ea_ref[...] + eb_ref[...]
    mine = pl.multiple_of(core * half, half)
    other = pl.multiple_of((1 - core) * half, half)
    for chunk in range(chunks):
        copies[chunk].wait()
        copies[chunks + chunk].wait()
        for row in range(count):
            p = chunk * count + row
            gap = base - occ_ref[pair_ref[p, 0]] - occ_ref[pair_ref[p, 1]]
            tile = tiles[chunk][row].astype(jnp.float32)
            swapped = mirrors[chunk][row].T.astype(jnp.float32)
            work_ref[p % 2] = ((2.0 * tile - swapped) / gap).astype(jnp.bfloat16)
            keep_ref[p] = work_ref[p % 2, pl.ds(mine, half), :]
            send_ref[p] = work_ref[p % 2, pl.ds(other, half), :]


def amplitude(core, occ_energy, pair_list, ea, eb, tiles, mirrors, ready):
    pairs = pair_list.shape[0]
    rows = tiles[0].shape[1]
    smem = pl.BlockSpec(memory_space=pltpu.SMEM)
    vmem = pl.BlockSpec(memory_space=pltpu.VMEM)
    hbm = pl.BlockSpec(memory_space=pl.ANY)
    chunks = len(tiles)
    shape = jax.ShapeDtypeStruct((pairs, rows // 2, rows), jnp.bfloat16)
    return pl.pallas_call(
        lambda *refs: amplitude_kernel(chunks, *refs),
        in_specs=[smem] * (3 + len(ready)) + [vmem] * 2 + [hbm] * (2 * chunks),
        out_specs=[vmem, vmem],
        out_shape=[shape, shape],
        scratch_shapes=[
            pltpu.VMEM((2, rows, rows), jnp.bfloat16),
            pltpu.VMEM((2 * chunks,) + tiles[0].shape, jnp.bfloat16),
            pltpu.SemaphoreType.DMA((2 * chunks,)),
        ],
        cost_estimate=pl.CostEstimate(
            flops=10 * pairs * rows * rows, bytes_accessed=6 * pairs * rows * rows, transcendentals=0
        ),
        name="amplitude",
    )(
        core, occ_energy, pair_list, *ready, ea.reshape(rows, 1), eb.reshape(1, rows), *tiles, *mirrors
    )


def contract_kernel(low, slot_ref, occ_ref, amp0, amp1, right0, right1, *refs):
    out_refs, (amp_ref, amp_sems, buf_ref, acc_ref, stage_ref, in_sems, out_sems) = refs[:-7], refs[-7:]
    pairs = amp0.shape[0]
    amps = fetch((amp0, amp1), amp_ref, amp_sems)
    dom_blocks = slot_ref.shape[2]
    sides = ((amp0, right0), (amp1, right1))

    def taken(side, p):
        return (occ_ref[side, p] >= low) & (occ_ref[side, p] < low + SPLIT)

    def load(side, p):
        return pltpu.make_async_copy(
            sides[side][1].at[p], buf_ref.at[side, p], in_sems.at[side, p]
        )

    for side in range(2):

        @pl.loop(0, pairs)
        def _(p):
            @pl.when(taken(side, p))
            def _():
                load(side, p).start()

    acc_ref[...] = jnp.zeros_like(acc_ref)
    for side in range(2):
        amps[side].wait()

        @pl.loop(0, pairs)
        def _(p):
            @pl.when(taken(side, p))
            def _():
                load(side, p).wait()
                part = jnp.dot(amp_ref[side, p], buf_ref[side, p], preferred_element_type=jnp.float32)
                for k in range(dom_blocks):
                    slot = slot_ref[side, p, k] + occ_ref[side, p] - low
                    acc_ref[slot] += part[:, k * BLOCK : (k + 1) * BLOCK]

    group = out_refs[0].shape[1]
    copies = []
    for out_ref in out_refs:
        for block in range(out_ref.shape[0]):
            place = len(copies)
            stage_ref[place] = acc_ref[place * group : (place + 1) * group].astype(stage_ref.dtype)
            copy = pltpu.make_async_copy(
                stage_ref.at[place], out_ref.at[block], out_sems.at[place]
            )
            copy.start()
            copies.append(copy)
    for copy in copies:
        copy.wait()


def contract(slots, orbitals, amp0, amp1, right0, right1, low, outs):
    pairs, half, rows = amp0.shape
    dom = right0.shape[2]
    total = AUX_BLK * SPLIT
    places = sum(outs)
    group = total // places
    smem = pl.BlockSpec(memory_space=pltpu.SMEM)
    hbm = pl.BlockSpec(memory_space=pl.ANY)
    return pl.pallas_call(
        lambda *refs: contract_kernel(low, *refs),
        in_specs=[smem, smem, hbm, hbm, hbm, hbm],
        out_specs=[hbm] * len(outs),
        out_shape=[jax.ShapeDtypeStruct((n, group, half, BLOCK), jnp.bfloat16) for n in outs],
        scratch_shapes=[
            pltpu.VMEM((2, pairs, half, rows), jnp.bfloat16),
            pltpu.SemaphoreType.DMA((2,)),
            pltpu.VMEM((2, pairs, rows, dom), jnp.bfloat16),
            pltpu.VMEM((total, half, BLOCK), jnp.float32),
            pltpu.VMEM((places, group, half, BLOCK), jnp.bfloat16),
            pltpu.SemaphoreType.DMA((2, pairs)),
            pltpu.SemaphoreType.DMA((places,)),
        ],
        cost_estimate=pl.CostEstimate(
            flops=2 * pairs * half * rows * dom,
            bytes_accessed=2 * pairs * rows * dom + 2 * total * half * BLOCK,
            transcendentals=0,
        ),
        compiler_params=pltpu.CompilerParams(vmem_limit_bytes=60 << 20),
        name="contract",
    )(slots, orbitals, amp0, amp1, right0, right1)


def add_kernel(places, own0, other0, own1, other1, *refs):
    outs, (own_buf, other_buf, kept_buf, sent_buf, in_sems, out_sems) = refs[:-6], refs[-6:]
    kept_ref, sent = outs[0], outs[1:]
    count = own_buf.shape[1]
    half = count // 2
    order = [(variant, n) for n in [*range(half, count), *range(half)] for variant in range(2)]
    loads = {}
    for variant, n in order:
        own, other = ((own0, other0), (own1, other1))[variant]
        own_at, other_at = places[2 * variant], places[2 * variant + 1]
        loads[variant, n] = [
            pltpu.make_async_copy(
                own.at[own_at * count + n], own_buf.at[variant, n], in_sems.at[0, variant, n]
            ),
            pltpu.make_async_copy(
                other.at[other_at * count + n], other_buf.at[variant, n], in_sems.at[1, variant, n]
            ),
        ]
        for copy in loads[variant, n]:
            copy.start()
    stores = []
    for variant, n in order:
        for copy in loads[variant, n]:
            copy.wait()
        total = own_buf[variant, n].astype(jnp.float32) + other_buf[variant, n].astype(jnp.float32)
        if n < half:
            kept_buf[variant, n] = total
            source, target = kept_buf.at[variant, n], kept_ref.at[variant, n]
        else:
            sent_buf[variant, n - half] = total.astype(jnp.bfloat16)
            source = sent_buf.at[variant, n - half]
            if len(sent) == 2:
                target = sent[variant].at[n - half]
            else:
                target = sent[0].at[variant * half + n - half]
        store = pltpu.make_async_copy(source, target, out_sems.at[variant, n])
        store.start()
        stores.append(store)
    for store in stores:
        store.wait()


def add_halves(owns, others, count, joined):
    group, half, width = owns[0][0].shape[-3:]
    flat = [pair for pairs in zip(owns, others) for pair in pairs]
    arrays = [array.reshape((-1, group, half, width)) for array, _ in flat]
    places = [at for _, at in flat]
    sent = [count] if joined else [count // 2] * 2
    hbm = pl.BlockSpec(memory_space=pl.ANY)
    return pl.pallas_call(
        lambda *refs: add_kernel(places, *refs),
        in_specs=[hbm] * 4,
        out_specs=[hbm] * (1 + len(sent)),
        out_shape=[jax.ShapeDtypeStruct((2, count // 2, group, half, width), jnp.float32)]
        + [jax.ShapeDtypeStruct((n, group, half, width), jnp.bfloat16) for n in sent],
        scratch_shapes=[
            pltpu.VMEM((2, count, group, half, width), arrays[0].dtype),
            pltpu.VMEM((2, count, group, half, width), arrays[1].dtype),
            pltpu.VMEM((2, count // 2, group, half, width), jnp.float32),
            pltpu.VMEM((2, count // 2, group, half, width), jnp.bfloat16),
            pltpu.SemaphoreType.DMA((2, 2, count)),
            pltpu.SemaphoreType.DMA((2, count)),
        ],
        cost_estimate=pl.CostEstimate(
            flops=2 * count * group * half * width,
            bytes_accessed=14 * count * group * half * width,
            transcendentals=0,
        ),
        name="add_halves",
    )(*arrays)


def last_add_kernel(core_ref, kept_in, other0, other1, *refs):
    outs, (kept_buf, other_buf, sum_buf, sent_buf, in_sems, out_sems) = refs[:4], refs[4:]
    core = core_ref[0]
    loads = []
    for variant, other in enumerate((other0, other1)):
        loads.append(
            [
                pltpu.make_async_copy(
                    kept_in.at[variant], kept_buf.at[variant], in_sems.at[0, variant]
                ),
                pltpu.make_async_copy(other, other_buf.at[variant], in_sems.at[1, variant]),
            ]
        )
        for copy in loads[variant]:
            copy.start()
    for variant in range(2):
        for copy in loads[variant]:
            copy.wait()
        sent_buf[variant] = (
            kept_buf[variant, 1] + other_buf[variant, 1].astype(jnp.float32)
        ).astype(jnp.bfloat16)
        sum_buf[variant] = kept_buf[variant, 0] + other_buf[variant, 0].astype(jnp.float32)

    def stores(where):
        own_ref, swap_ref, same_ref, cross_ref = outs
        return [
            pltpu.make_async_copy(sent_buf.at[where], same_ref, out_sems.at[0]),
            pltpu.make_async_copy(sent_buf.at[1 - where], cross_ref, out_sems.at[1]),
            pltpu.make_async_copy(sum_buf.at[where], own_ref, out_sems.at[2]),
            pltpu.make_async_copy(sum_buf.at[1 - where], swap_ref, out_sems.at[3]),
        ]

    for where in range(2):

        @pl.when(core == where)
        def _():
            for copy in stores(where):
                copy.start()
            for copy in stores(where):
                copy.wait()


def last_add(core, kept, other0, other1):
    group, half, width = kept.shape[-3:]
    shape = (group, half, width)
    hbm = pl.BlockSpec(memory_space=pl.ANY)
    return pl.pallas_call(
        last_add_kernel,
        in_specs=[pl.BlockSpec(memory_space=pltpu.SMEM)] + [hbm] * 3,
        out_specs=[hbm] * 4,
        out_shape=[jax.ShapeDtypeStruct(shape, jnp.float32)] * 2
        + [jax.ShapeDtypeStruct(shape, jnp.bfloat16)] * 2,
        scratch_shapes=[
            pltpu.VMEM((2, 2) + shape, jnp.float32),
            pltpu.VMEM((2, 2) + shape, jnp.bfloat16),
            pltpu.VMEM((2,) + shape, jnp.float32),
            pltpu.VMEM((2,) + shape, jnp.bfloat16),
            pltpu.SemaphoreType.DMA((2, 2)),
            pltpu.SemaphoreType.DMA((4,)),
        ],
        cost_estimate=pl.CostEstimate(
            flops=kept.size, bytes_accessed=10 * kept.size, transcendentals=0
        ),
        name="last_add",
    )(core, kept, other0, other1)


def finish_kernel(core_ref, *refs):
    ins, (out_ref, kept_buf, far_buf, out_buf, in_sems, out_sems) = refs[:8], refs[8:]
    core = core_ref[0]
    blocks = PER_OWNER // 2
    half = kept_buf.shape[-2]
    loads = []
    for part in range(2):
        for side in range(2):
            at = 2 * part + side
            loads += [
                pltpu.make_async_copy(ins[4 * part + side], kept_buf.at[at], in_sems.at[0, at]),
                pltpu.make_async_copy(ins[4 * part + 2 + side], far_buf.at[at], in_sems.at[1, at]),
            ]
    for copy in loads:
        copy.start()
    for copy in loads:
        copy.wait()

    def write(block, order):
        rows = slice(block * BLOCK, (block + 1) * BLOCK)
        for part in range(2):
            for occ in range(SPLIT):
                row = block * SPLIT + occ
                for side in range(2):
                    at = 2 * part + (side if order == 0 else 1 - side)
                    total = kept_buf[at, row] + far_buf[at, row].astype(jnp.float32)
                    out_buf[rows, part * SPLIT + occ, side * half : (side + 1) * half] = total.T

    stores = []
    for block in range(blocks):

        @pl.when(core == 0)
        def _():
            write(block, 0)

        @pl.when(core != 0)
        def _():
            write(block, 1)

        rows = slice(block * BLOCK, (block + 1) * BLOCK)
        store = pltpu.make_async_copy(out_buf.at[rows], out_ref.at[rows], out_sems.at[block])
        store.start()
        stores.append(store)
    for store in stores:
        store.wait()


def finish(core, low, high):
    group, half, width = low[0].shape
    blocks = PER_OWNER // 2
    hbm = pl.BlockSpec(memory_space=pl.ANY)
    shape = jax.ShapeDtypeStruct((blocks * width, 2 * SPLIT, 2 * half), jnp.float32)
    return pl.pallas_call(
        finish_kernel,
        in_specs=[pl.BlockSpec(memory_space=pltpu.SMEM)] + [hbm] * 8,
        out_specs=hbm,
        out_shape=shape,
        scratch_shapes=[
            pltpu.VMEM((4, group, half, width), jnp.float32),
            pltpu.VMEM((4, group, half, width), jnp.bfloat16),
            pltpu.VMEM(shape.shape, jnp.float32),
            pltpu.SemaphoreType.DMA((2, 4)),
            pltpu.SemaphoreType.DMA((blocks,)),
        ],
        cost_estimate=pl.CostEstimate(
            flops=shape.size, bytes_accessed=10 * shape.size, transcendentals=0
        ),
        name="finish",
    )(core, *low, *high)


def last_steps(same, cross, bits):
    pairs_same, pairs_cross = [], []
    for vb, core in itertools.product(range(8), range(2)):
        pairs_same.append((vb * 2 + core, (vb ^ bits[core]) * 2 + core))
        pairs_cross.append((vb * 2 + core, (vb ^ bits[1 - core]) * 2 + 1 - core))
    axes = ("vb", "pair")
    return lax.ppermute(same, axes, pairs_same), lax.ppermute(cross, axes, pairs_cross)


def step_y(value, bits):
    return lax.ppermute(value, "vb", [(j, j ^ bits) for j in range(8)])


def swap_z(value):
    return step_y(value, 4)


def program(left_fit, right_fit, occ_energy, virt_energy, pair_list, domain_blocks):
    pairs, rows, _ = left_fit.shape
    dom_blocks = domain_blocks.shape[1]
    core = lax.axis_index("pair")
    ea = lax.dynamic_slice_in_dim(virt_energy, lax.axis_index("va") * rows, rows)
    eb = lax.dynamic_slice_in_dim(virt_energy, lax.axis_index("vb") * rows, rows)
    swap = [(0, 1), (1, 0)]
    vb = lax.axis_index("vb")
    table = jnp.concatenate([domain_blocks, pair_list[:, :1]], axis=1)
    both = jnp.stack([table, lax.ppermute(table, "pair", swap)])
    blocks, orbitals = both[:, :, :dom_blocks], both[:, :, dom_blocks]
    apart = (blocks // PER_OWNER) ^ vb
    apart_z, apart_y = apart // 4, apart % 4
    variant = blocks % PER_OWNER // 2
    near = jnp.where(variant == 0, 3, 1)
    code = jnp.where(
        apart_y == 0, 0, jnp.where(apart_y == near, 1, jnp.where(apart_y == 2, 3, 2))
    )
    inner = blocks % 2
    slots_high = (((apart_z * 2 + variant) * 4 + code) * 2 + inner) * SPLIT
    slots_low = (((variant * 4 + code) * 2 + apart_z) * 2 + inner) * SPLIT
    other_right = lax.ppermute(right_fit, "pair", swap)
    count = pairs // CHUNKS
    tiles = []
    for piece in range(CHUNKS):
        tiles += coulomb(left_fit, right_fit, piece * count, count, 1, tuple(tiles[-1:]))
    mirrors = []
    for piece, tile in enumerate(tiles):
        out, back = detour_pairs(piece)
        mid = lax.ppermute(tile, AXES, out)
        mirrors.append(lax.ppermute(mid, AXES, back))
    me = core.reshape(1).astype(jnp.int32)
    ready = (slots_high, slots_low, orbitals)
    keep, send = amplitude(me, occ_energy, pair_list, ea, eb, tiles, mirrors, ready)
    other_amp = lax.ppermute(send, "pair", swap)
    operands = (orbitals, keep, other_amp, right_fit, other_right)
    stay0, stay1, cross = contract(slots_high, *operands, SPLIT, (4, 4, 8))
    crossed = swap_z(cross)
    low0, sent0, low1, sent1 = contract(slots_low, *operands, 0, (4, 4, 4, 4))
    got0, got1 = step_y(sent0, 1), step_y(sent1, 3)
    kept_low, sent0, sent1 = add_halves(
        [(low0, 0), (low1, 0)], [(got0, 0), (got1, 0)], 4, False
    )
    got0, got1 = step_y(sent0, 3), step_y(sent1, 1)
    kept_high, high0, high1 = add_halves(
        [(stay0, 0), (stay1, 0)], [(crossed, 0), (crossed, 1)], 4, False
    )
    more0, more1 = step_y(high0, 1), step_y(high1, 3)
    own_low, swap_low, *sent = last_add(me, kept_low, got0, got1)
    arrived = last_steps(*sent, (4, 4))
    low = [own_low, lax.ppermute(swap_low, "pair", swap), *arrived]
    own_high, swap_high, *sent = last_add(me, kept_high, more0, more1)
    high = [own_high, lax.ppermute(swap_high, "pair", swap), *last_steps(*sent, (3, 1))]
    return finish(me, low, high)


def solution(mesh):
    return jax.shard_map(
        program,
        mesh=mesh,
        in_specs=(
            P("pair", "va", None),
            P("pair", "vb", None),
            P(),
            P(),
            P("pair", None),
            P("pair", None),
        ),
        out_specs=P(("vb", "pair"), None, "va"),
        check_vma=False,
    )
```

profile of v0, /device:TPU:0, one launch (start us, length us, event | category | flops | bytes accessed | tf_op | source)
XLA Modules:
  0.0 213.4 jit_solution(2947020224542878254)
XLA Ops:
  0.0 3.8 %coulomb.5.refs_2_.refs_8_ = bf16[3,256,256]{2,1,0:T(8,128)(2,1)} custom-call(bf16[15,256,1536]{2,1,0:T(8,128)(2,1)} %refs_0_.9, bf16[15,256,1536]{2,1,0:T(8,128)(2,1)} %refs_4_.3), custom_call_target="tpu_custom_call" | custom-call | flops 603979776 | bytes 5111808 | tf_op jit(solution)/shard_map/coulomb/pallas_call | solution.py:68
  3.9 3.9 %coulomb.6.refs_2_.refs_9_ = bf16[3,256,256]{2,1,0:T(8,128)(2,1)} custom-call(bf16[15,256,1536]{2,1,0:T(8,128)(2,1)} %refs_0_.9, bf16[15,256,1536]{2,1,0:T(8,128)(2,1)} %refs_4_.3, bf16[3,256,256]{2,1,0:T(8,128)(2,1)} %coulomb.5.refs_2_.refs_8_), custom_call_target="tpu_custom_call" | custom-call | flops 603979776 | bytes 5111808 | tf_op jit(solution)/shard_map/coulomb/pallas_call | solution.py:68
  7.7 3.8 %coulomb.7.refs_2_.refs_10_ = bf16[3,256,256]{2,1,0:T(8,128)(2,1)} custom-call(bf16[15,256,1536]{2,1,0:T(8,128)(2,1)} %refs_0_.9, bf16[15,256,1536]{2,1,0:T(8,128)(2,1)} %refs_4_.3, bf16[3,256,256]{2,1,0:T(8,128)(2,1)} %coulomb.6.refs_2_.refs_9_), custom_call_target="tpu_custom_call" | custom-call | flops 603979776 | bytes 5111808 | tf_op jit(solution)/shard_map/coulomb/pallas_call | solution.py:68
  11.5 3.8 %coulomb.8.refs_2_.refs_11_ = bf16[3,256,256]{2,1,0:T(8,128)(2,1)} custom-call(bf16[15,256,1536]{2,1,0:T(8,128)(2,1)} %refs_0_.9, bf16[15,256,1536]{2,1,0:T(8,128)(2,1)} %refs_4_.3, bf16[3,256,256]{2,1,0:T(8,128)(2,1)} %coulomb.7.refs_2_.refs_10_), custom_call_target="tpu_custom_call" | custom-call | flops 603979776 | bytes 5111808 | tf_op jit(solution)/shard_map/coulomb/pallas_call | solution.py:68
  15.5 3.9 %coulomb.9.refs_12_ = bf16[3,256,256]{2,1,0:T(8,128)(2,1)} custom-call(bf16[15,256,1536]{2,1,0:T(8,128)(2,1)} %refs_0_.9, bf16[15,256,1536]{2,1,0:T(8,128)(2,1)} %refs_4_.3, bf16[3,256,256]{2,1,0:T(8,128)(2,1)} %coulomb.8.refs_2_.refs_11_), custom_call_target="tpu_custom_call" | custom-call | flops 603979776 | bytes 5111808 | tf_op jit(solution)/shard_map/coulomb/pallas_call | solution.py:68
  19.4 4.7 %collective-permute-start.9 = (bf16[3,256,256]{2,1,0:T(8,128)(2,1)}, bf16[3,256,256]{2,1,0:T(8,128)(2,1)}, u32[]{:S(2)}, u32[]{:S(2)}) collective-permute-start(bf16[3,256,256]{2,1,0:T(8,128)(2,1)} %coulomb.9.refs_12_), channel_id=1, source_target_pairs={{0,12},{1,57},{8,20},{9,33},{16,28},{17,41},{24,4},{25,49},{2,14},... | collective-permute-start | bytes 1179656 | tf_op jit(solution)/shard_map/ppermute | solution.py:491
  24.1 4.1 %collective-permute-start.7 = (bf16[3,256,256]{2,1,0:T(8,128)(2,1)S(1)}, bf16[3,256,256]{2,1,0:T(8,128)(2,1)S(1)}, u32[]{:S(2)}, u32[]{:S(2)}) collective-permute-start(bf16[3,256,256]{2,1,0:T(8,128)(2,1)S(1)} %copy-done.5), channel_id=1, source_target_pairs={{0,104},{1,69},{8,112},{9,77},{16,120},{17,85},{24,96},{25,93},{2,... | collective-permute-start | bytes 1179656 | tf_op jit(solution)/shard_map/ppermute | solution.py:491
  30.9 1.7 collective-permute-start.3
  33.9 8.2 %collective-permute-start.1 = (bf16[3,256,256]{2,1,0:T(8,128)(2,1)S(1)}, bf16[3,256,256]{2,1,0:T(8,128)(2,1)}, u32[]{:S(2)}, u32[]{:S(2)}) collective-permute-start(bf16[3,256,256]{2,1,0:T(8,128)(2,1)S(1)} %copy-done.2), channel_id=1, source_target_pairs={{0,30},{1,99},{8,6},{9,107},{16,14},{17,115},{24,22},{25,123},{2,2... | collective-permute-start | bytes 1179656 | tf_op jit(solution)/shard_map/ppermute | solution.py:491
  43.7 6.2 %collective-permute-done.5 = bf16[3,256,256]{2,1,0:T(8,128)(2,1)S(1)} collective-permute-done((bf16[3,256,256]{2,1,0:T(8,128)(2,1)S(1)}, bf16[3,256,256]{2,1,0:T(8,128)(2,1)S(1)}, u32[]{:S(2)}, u32[]{:S(2)}) %collective-permute-start.5) | collective-permute-done | bytes 393248 | tf_op jit(solution)/shard_map/ppermute | solution.py:491
  50.0 10.4 %collective-permute-start.8 = (bf16[3,256,256]{2,1,0:T(8,128)(2,1)S(1)}, bf16[3,256,256]{2,1,0:T(8,128)(2,1)S(1)}, u32[]{:S(2)}, u32[]{:S(2)}) collective-permute-start(bf16[3,256,256]{2,1,0:T(8,128)(2,1)S(1)} %collective-permute-done.7), channel_id=1, source_target_pairs={{104,0},{69,1},{112,64},{77,65},{120,2},{85,3},{96,66},{93,67},{10... | collective-permute-start | bytes 1179656 | tf_op jit(solution)/shard_map/ppermute | solution.py:492
  60.4 2.6 %collective-permute-done.1 = bf16[3,256,256]{2,1,0:T(8,128)(2,1)} collective-permute-done((bf16[3,256,256]{2,1,0:T(8,128)(2,1)S(1)}, bf16[3,256,256]{2,1,0:T(8,128)(2,1)}, u32[]{:S(2)}, u32[]{:S(2)}) %collective-permute-start.1) | collective-permute-done | bytes 393248 | tf_op jit(solution)/shard_map/ppermute | solution.py:491
  62.9 10.0 %collective-permute-start.4 = (bf16[3,256,256]{2,1,0:T(8,128)(2,1)S(1)}, bf16[3,256,256]{2,1,0:T(8,128)(2,1)S(1)}, u32[]{:S(2)}, u32[]{:S(2)}) collective-permute-start(bf16[3,256,256]{2,1,0:T(8,128)(2,1)S(1)} %collective-permute-done.3), channel_id=1, source_target_pairs={{38,0},{11,1},{46,64},{19,65},{54,2},{27,3},{62,66},{3,67},{32,16}... | collective-permute-start | bytes 1179656 | tf_op jit(solution)/shard_map/ppermute | solution.py:492
  73.0 2.6 %collective-permute-start.2 = (bf16[3,256,256]{2,1,0:T(8,128)(2,1)}, bf16[3,256,256]{2,1,0:T(8,128)(2,1)S(1)}, u32[]{:S(2)}, u32[]{:S(2)}) collective-permute-start(bf16[3,256,256]{2,1,0:T(8,128)(2,1)} %collective-permute-done.1), channel_id=1, source_target_pairs={{30,0},{99,1},{6,64},{107,65},{14,2},{115,3},{22,66},{123,67},{24,... | collective-permute-start | bytes 1179656 | tf_op jit(solution)/shard_map/ppermute | solution.py:492
  81.0 7.5 %collective-permute-done.2.refs_13_ = bf16[3,256,256]{2,1,0:T(8,128)(2,1)S(1)} collective-permute-done((bf16[3,256,256]{2,1,0:T(8,128)(2,1)}, bf16[3,256,256]{2,1,0:T(8,128)(2,1)S(1)}, u32[]{:S(2)}, u32[]{:S(2)}) %collective-permute-start.2) | collective-permute-done | bytes 393248 | tf_op jit(solution)/shard_map/ppermute | solution.py:492
  89.3 5.7 %amplitude.1 = (bf16[15,128,256]{2,1,0:T(8,128)(2,1)}, bf16[15,128,256]{2,1,0:T(8,128)(2,1)}) custom-call(s32[1]{0:T(128)} %bitcast.refs_0_.core_ref, f32[8]{0:T(128)} %refs_1_.11, s32[15,2]{1,0:T(8,128)} %copy.10.refs_2_, s32[2,15,12]{2,1,0:T(8,128)} %get-tuple-element.51.refs_3_.refs_0_, s32[2,15,12]{2,1,0:T(8,128)} %get-tuple-element.52.refs_4_.refs_0_, ...), custom_call_target="tpu_custom_call" | custom-call | flops 9830400 | bytes 5898240 | tf_op jit(solution)/shard_map/amplitude/pallas_call | solution.py:132
  95.1 2.8 %collective-permute-done.11.refs_3_ = bf16[15,128,256]{2,1,0:T(8,128)(2,1)S(1)} collective-permute-done((bf16[15,128,256]{2,1,0:T(8,128)(2,1)}, bf16[15,128,256]{2,1,0:T(8,128)(2,1)S(1)}, u32[]{:S(2)}, u32[]{:S(2)}) %collective-permute-start.11) | collective-permute-done | bytes 983072 | tf_op jit(solution)/shard_map/ppermute | solution.py:496
  98.8 7.8 %contract.3 = (bf16[4,8,128,128]{3,2,1,0:T(8,128)(2,1)}, bf16[4,8,128,128]{3,2,1,0:T(8,128)(2,1)}, bf16[8,8,128,128]{3,2,1,0:T(8,128)(2,1)}) custom-call(s32[2,15,12]{2,1,0:T(8,128)} %get-tuple-element.51.refs_3_.refs_0_, s32[2,15]{1,0:T(2,128)} %fusion.2.refs_5_.refs_1_, bf16[15,128,256]{2,1,0:T(8,128)(2,1)} %get-tuple-element.28.refs_2_, ...), custom_call_target="tpu_custom_call" | custom-call | flops 1509949440 | bytes 15990784 | tf_op jit(solution)/shard_map/contract/pallas_call | solution.py:211
  106.6 18.6 %collective-permute-start.20 = (bf16[8,8,128,128]{3,2,1,0:T(8,128)(2,1)}, bf16[8,8,128,128]{3,2,1,0:T(8,128)(2,1)S(1)}, u32[]{:S(2)}, u32[]{:S(2)}) collective-permute-start(bf16[8,8,128,128]{3,2,1,0:T(8,128)(2,1)} %get-tuple-element.42), channel_id=1, source_target_pairs={{0,8},{2,10},{4,12},{6,14},{8,0},{10,2},{12,4},{14,6},{1,9},{3,11}... | collective-permute-start | bytes 6291464 | tf_op jit(solution)/shard_map/ppermute | solution.py:455
  125.2 11.9 %contract.2 = (bf16[4,8,128,128]{3,2,1,0:T(8,128)(2,1)}, bf16[4,8,128,128]{3,2,1,0:T(8,128)(2,1)}, bf16[4,8,128,128]{3,2,1,0:T(8,128)(2,1)}, bf16[4,8,128,128]{3,2,1,0:T(8,128)(2,1)}) custom-call(s32[2,15,12]{2,1,0:T(8,128)} %get-tuple-element.52.refs_4_.refs_0_, s32[2,15]{1,0:T(2,128)} %fusion.2.refs_5_.refs_1_, ...), custom_call_target="tpu_custom_call" | custom-call | flops 1509949440 | bytes 15990784 | tf_op jit(solution)/shard_map/contract/pallas_call | solution.py:211
  137.3 25.1 %collective-permute-done.13.refs_1_ = bf16[4,8,128,128]{3,2,1,0:T(8,128)(2,1)S(1)} collective-permute-done((bf16[4,8,128,128]{3,2,1,0:T(8,128)(2,1)}, bf16[4,8,128,128]{3,2,1,0:T(8,128)(2,1)S(1)}, u32[]{:S(2)}, u32[]{:S(2)}) %collective-permute-start.13) | collective-permute-done | bytes 1048608 | tf_op jit(solution)/shard_map/ppermute | solution.py:455
  163.8 3.4 %add_halves.2 = (f32[2,2,8,128,128]{4,3,2,1,0:T(8,128)}, bf16[2,8,128,128]{3,2,1,0:T(8,128)(2,1)}, bf16[2,8,128,128]{3,2,1,0:T(8,128)(2,1)}) custom-call(bf16[4,8,128,128]{3,2,1,0:T(8,128)(2,1)} %get-tuple-element.30.refs_0_, bf16[4,8,128,128]{3,2,1,0:T(8,128)(2,1)} %copy-done.6, bf16[4,8,128,128]{3,2,1,0:T(8,128)(2,1)} %get-tuple-element.32.refs_2_, ...), custom_call_target="tpu_custom_call" | custom-call | flops 1048576 | bytes 7340032 | tf_op jit(solution)/shard_map/add_halves/pallas_call | solution.py:284
  168.1 3.4 %collective-permute-done.20.refs_1_.refs_3_ = bf16[8,8,128,128]{3,2,1,0:T(8,128)(2,1)S(1)} collective-permute-done((bf16[8,8,128,128]{3,2,1,0:T(8,128)(2,1)}, bf16[8,8,128,128]{3,2,1,0:T(8,128)(2,1)S(1)}, u32[]{:S(2)}, u32[]{:S(2)}) %collective-permute-start.20) | collective-permute-done | bytes 2097184 | tf_op jit(solution)/shard_map/ppermute | solution.py:455
  172.8 3.4 %add_halves.3 = (f32[2,2,8,128,128]{4,3,2,1,0:T(8,128)}, bf16[2,8,128,128]{3,2,1,0:T(8,128)(2,1)}, bf16[2,8,128,128]{3,2,1,0:T(8,128)(2,1)}) custom-call(bf16[4,8,128,128]{3,2,1,0:T(8,128)(2,1)} %get-tuple-element.41.refs_0_, bf16[8,8,128,128]{3,2,1,0:T(8,128)(2,1)} %copy-done, bf16[4,8,128,128]{3,2,1,0:T(8,128)(2,1)} %get-tuple-element.43.refs_2_, ...), custom_call_target="tpu_custom_call" | custom-call | flops 1048576 | bytes 7340032 | tf_op jit(solution)/shard_map/add_halves/pallas_call | solution.py:284
  177.5 5.8 %collective-permute-done.15.other0 = bf16[2,8,128,128]{3,2,1,0:T(8,128)(2,1)S(1)} collective-permute-done((bf16[2,8,128,128]{3,2,1,0:T(8,128)(2,1)}, bf16[2,8,128,128]{3,2,1,0:T(8,128)(2,1)S(1)}, u32[]{:S(2)}, u32[]{:S(2)}) %collective-permute-start.15) | collective-permute-done | bytes 524320 | tf_op jit(solution)/shard_map/ppermute | solution.py:455
  184.2 3.1 %last_add.2 = (f32[8,128,128]{2,1,0:T(8,128)}, f32[8,128,128]{2,1,0:T(8,128)}, bf16[8,128,128]{2,1,0:T(8,128)(2,1)}, bf16[8,128,128]{2,1,0:T(8,128)(2,1)}) custom-call(s32[1]{0:T(128)} %bitcast.refs_0_.core_ref, f32[2,2,8,128,128]{4,3,2,1,0:T(8,128)} %get-tuple-element.34.kept_in, bf16[2,8,128,128]{3,2,1,0:T(8,128)(2,1)} %copy-done.9, ...), custom_call_target="tpu_custom_call" | custom-call | flops 524288 | bytes 5242880 | tf_op jit(solution)/shard_map/last_add/pallas_call | solution.py:353
  187.5 4.4 %collective-permute-done.21.other0 = bf16[2,8,128,128]{3,2,1,0:T(8,128)(2,1)S(1)} collective-permute-done((bf16[2,8,128,128]{3,2,1,0:T(8,128)(2,1)}, bf16[2,8,128,128]{3,2,1,0:T(8,128)(2,1)S(1)}, u32[]{:S(2)}, u32[]{:S(2)}) %collective-permute-start.21) | collective-permute-done | bytes 524320 | tf_op jit(solution)/shard_map/ppermute | solution.py:455
  193.7 3.1 %last_add.3 = (f32[8,128,128]{2,1,0:T(8,128)}, f32[8,128,128]{2,1,0:T(8,128)}, bf16[8,128,128]{2,1,0:T(8,128)(2,1)}, bf16[8,128,128]{2,1,0:T(8,128)(2,1)}) custom-call(s32[1]{0:T(128)} %bitcast.refs_0_.core_ref, f32[2,2,8,128,128]{4,3,2,1,0:T(8,128)} %get-tuple-element.44.kept_in, bf16[2,8,128,128]{3,2,1,0:T(8,128)(2,1)} %copy-done.7, ...), custom_call_target="tpu_custom_call" | custom-call | flops 524288 | bytes 5242880 | tf_op jit(solution)/shard_map/last_add/pallas_call | solution.py:353
  197.5 1.9 collective-permute-start.24
  199.4 5.5 %collective-permute-done.19.refs_3_ = bf16[8,128,128]{2,1,0:T(8,128)(2,1)S(1)} collective-permute-done((bf16[8,128,128]{2,1,0:T(8,128)(2,1)S(1)}, bf16[8,128,128]{2,1,0:T(8,128)(2,1)S(1)}, u32[]{:S(2)}, u32[]{:S(2)}) %collective-permute-start.19) | collective-permute-done | bytes 262176 | tf_op jit(solution)/shard_map/ppermute | solution.py:451
  204.9 1.8 collective-permute-done.24.refs_6_
  209.0 4.2 %finish.1 = f32[256,8,256]{2,1,0:T(8,128)} custom-call(s32[1]{0:T(128)} %bitcast.refs_0_.core_ref, f32[8,128,128]{2,1,0:T(8,128)} %get-tuple-element.37.refs_0_, f32[8,128,128]{2,1,0:T(8,128)} %copy-done.11, bf16[8,128,128]{2,1,0:T(8,128)(2,1)} %copy-done.18, bf16[8,128,128]{2,1,0:T(8,128)(2,1)} %copy-done.19, f32[8,128,128]{2,1,0:T(8,128)} %get-tuple-element.47.refs_4_, ...), custom_call_target="tpu_custom_call" | custom-call | flops 524288 | bytes 5242880 | tf_op jit(solution)/shard_map/finish/pallas_call | solution.py:426
  (93 shorter events, 23.6 us)
Async XLA Ops:
  0.0 97.8 %collective-permute-start.12 = (bf16[15,256,1536]{2,1,0:T(8,128)(2,1)}, bf16[15,256,1536]{2,1,0:T(8,128)(2,1)}, u32[]{:S(2)}, u32[]{:S(2)}) collective-permute-start(bf16[15,256,1536]{2,1,0:T(8,128)(2,1)} %refs_4_.3), channel_id=1, source_target_pairs={{0,1},{1,0},{2,3},{3,2},{4,5},{5,4},{6,7},{7,6},{8,9},{9,8},{10,11... | collective-permute-start | bytes 35389448 | tf_op jit(solution)/shard_map/ppermute | solution.py:483
  15.4 12.9 %copy-start.22 = (s32[15,12]{1,0:T(8,128)S(1)}, s32[15,12]{1,0:T(8,128)}, u32[]{:S(2)}) copy-start(s32[15,12]{1,0:T(8,128)} %param.11) | copy-start | bytes 2164
  15.4 14.6 %copy-start.4 = (bf16[3,256,256]{2,1,0:T(8,128)(2,1)S(1)}, bf16[3,256,256]{2,1,0:T(8,128)(2,1)}, u32[]{:S(2)}) copy-start(bf16[3,256,256]{2,1,0:T(8,128)(2,1)} %coulomb.7.refs_2_.refs_10_) | copy-start | bytes 1179652
  15.4 15.4 %copy-start.3 = (bf16[3,256,256]{2,1,0:T(8,128)(2,1)S(1)}, bf16[3,256,256]{2,1,0:T(8,128)(2,1)}, u32[]{:S(2)}) copy-start(bf16[3,256,256]{2,1,0:T(8,128)(2,1)} %coulomb.6.refs_2_.refs_9_) | copy-start | bytes 1179652
  15.4 18.4 %copy-start.2 = (bf16[3,256,256]{2,1,0:T(8,128)(2,1)S(1)}, bf16[3,256,256]{2,1,0:T(8,128)(2,1)}, u32[]{:S(2)}) copy-start(bf16[3,256,256]{2,1,0:T(8,128)(2,1)} %coulomb.5.refs_2_.refs_8_) | copy-start | bytes 1179652
  15.4 60.1 %copy-start.23 = (s32[15,2]{0,1:T(2,128)S(1)}, s32[15,2]{0,1:T(2,128)}, u32[]{:S(2)}) copy-start(s32[15,2]{0,1:T(2,128)} %param.10) | copy-start | bytes 364
  19.4 14.5 %collective-permute-start.9 = (bf16[3,256,256]{2,1,0:T(8,128)(2,1)}, bf16[3,256,256]{2,1,0:T(8,128)(2,1)}, u32[]{:S(2)}, u32[]{:S(2)}) collective-permute-start(bf16[3,256,256]{2,1,0:T(8,128)(2,1)} %coulomb.9.refs_12_), channel_id=1, source_target_pairs={{0,12},{1,57},{8,20},{9,33},{16,28},{17,41},{24,4},{25,49},{2,14},... | collective-permute-start | bytes 1179656 | tf_op jit(solution)/shard_map/ppermute | solution.py:491
  24.1 18.0 %collective-permute-start.7 = (bf16[3,256,256]{2,1,0:T(8,128)(2,1)S(1)}, bf16[3,256,256]{2,1,0:T(8,128)(2,1)S(1)}, u32[]{:S(2)}, u32[]{:S(2)}) collective-permute-start(bf16[3,256,256]{2,1,0:T(8,128)(2,1)S(1)} %copy-done.5), channel_id=1, source_target_pairs={{0,104},{1,69},{8,112},{9,77},{16,120},{17,85},{24,96},{25,93},{2,... | collective-permute-start | bytes 1179656 | tf_op jit(solution)/shard_map/ppermute | solution.py:491
  28.4 2.5 %collective-permute-start = (s32[15,13]{1,0:T(8,128)S(1)}, s32[15,13]{1,0:T(8,128)S(1)}, u32[]{:S(2)}, u32[]{:S(2)}) collective-permute-start(s32[15,13]{1,0:T(8,128)S(1)} %pad_add_fusion.1), channel_id=1, source_target_pairs={{0,1},{1,0},{2,3},{3,2},{4,5},{5,4},{6,7},{7,6},{8,9},{9,8},{10,11... | collective-permute-start | bytes 2348 | tf_op jit(solution)/shard_map/ppermute | solution.py:471
  30.0 19.9 %collective-permute-start.5 = (bf16[3,256,256]{2,1,0:T(8,128)(2,1)S(1)}, bf16[3,256,256]{2,1,0:T(8,128)(2,1)S(1)}, u32[]{:S(2)}, u32[]{:S(2)}) collective-permute-start(bf16[3,256,256]{2,1,0:T(8,128)(2,1)S(1)} %copy-done.4), channel_id=1, source_target_pairs={{0,28},{1,49},{8,4},{9,57},{16,12},{17,33},{24,20},{25,41},{2,30},... | collective-permute-start | bytes 1179656 | tf_op jit(solution)/shard_map/ppermute | solution.py:491
  30.9 29.5 %collective-permute-start.3 = (bf16[3,256,256]{2,1,0:T(8,128)(2,1)S(1)}, bf16[3,256,256]{2,1,0:T(8,128)(2,1)S(1)}, u32[]{:S(2)}, u32[]{:S(2)}) collective-permute-start(bf16[3,256,256]{2,1,0:T(8,128)(2,1)S(1)} %copy-done.3), channel_id=1, source_target_pairs={{0,38},{1,11},{8,46},{9,19},{16,54},{17,27},{24,62},{25,3},{2,32},... | collective-permute-start | bytes 1179656 | tf_op jit(solution)/shard_map/ppermute | solution.py:491
  33.9 29.0 %collective-permute-start.1 = (bf16[3,256,256]{2,1,0:T(8,128)(2,1)S(1)}, bf16[3,256,256]{2,1,0:T(8,128)(2,1)}, u32[]{:S(2)}, u32[]{:S(2)}) collective-permute-start(bf16[3,256,256]{2,1,0:T(8,128)(2,1)S(1)} %copy-done.2), channel_id=1, source_target_pairs={{0,30},{1,99},{8,6},{9,107},{16,14},{17,115},{24,22},{25,123},{2,2... | collective-permute-start | bytes 1179656 | tf_op jit(solution)/shard_map/ppermute | solution.py:491
  42.1 30.9 %collective-permute-start.10 = (bf16[3,256,256]{2,1,0:T(8,128)(2,1)}, bf16[3,256,256]{2,1,0:T(8,128)(2,1)S(1)}, u32[]{:S(2)}, u32[]{:S(2)}) collective-permute-start(bf16[3,256,256]{2,1,0:T(8,128)(2,1)} %collective-permute-done.9), channel_id=1, source_target_pairs={{12,0},{57,1},{20,64},{33,65},{28,2},{41,3},{4,66},{49,67},{14,16}... | collective-permute-start | bytes 1179656 | tf_op jit(solution)/shard_map/ppermute | solution.py:492
  50.0 30.0 %collective-permute-start.8 = (bf16[3,256,256]{2,1,0:T(8,128)(2,1)S(1)}, bf16[3,256,256]{2,1,0:T(8,128)(2,1)S(1)}, u32[]{:S(2)}, u32[]{:S(2)}) collective-permute-start(bf16[3,256,256]{2,1,0:T(8,128)(2,1)S(1)} %collective-permute-done.7), channel_id=1, source_target_pairs={{104,0},{69,1},{112,64},{77,65},{120,2},{85,3},{96,66},{93,67},{10... | collective-permute-start | bytes 1179656 | tf_op jit(solution)/shard_map/ppermute | solution.py:492
  60.4 19.6 %collective-permute-start.6 = (bf16[3,256,256]{2,1,0:T(8,128)(2,1)S(1)}, bf16[3,256,256]{2,1,0:T(8,128)(2,1)S(1)}, u32[]{:S(2)}, u32[]{:S(2)}) collective-permute-start(bf16[3,256,256]{2,1,0:T(8,128)(2,1)S(1)} %collective-permute-done.5), channel_id=1, source_target_pairs={{28,0},{49,1},{4,64},{57,65},{12,2},{33,3},{20,66},{41,67},{30,16}... | collective-permute-start | bytes 1179656 | tf_op jit(solution)/shard_map/ppermute | solution.py:492
  62.9 18.1 %collective-permute-start.4 = (bf16[3,256,256]{2,1,0:T(8,128)(2,1)S(1)}, bf16[3,256,256]{2,1,0:T(8,128)(2,1)S(1)}, u32[]{:S(2)}, u32[]{:S(2)}) collective-permute-start(bf16[3,256,256]{2,1,0:T(8,128)(2,1)S(1)} %collective-permute-done.3), channel_id=1, source_target_pairs={{38,0},{11,1},{46,64},{19,65},{54,2},{27,3},{62,66},{3,67},{32,16}... | collective-permute-start | bytes 1179656 | tf_op jit(solution)/shard_map/ppermute | solution.py:492
  73.0 15.6 %copy-start.13 = (bf16[3,256,256]{2,1,0:T(8,128)(2,1)}, bf16[3,256,256]{2,1,0:T(8,128)(2,1)S(1)}, u32[]{:S(2)}) copy-start(bf16[3,256,256]{2,1,0:T(8,128)(2,1)S(1)} %collective-permute-done.10.refs_17_) | copy-start | bytes 1179652
  73.0 15.5 %collective-permute-start.2 = (bf16[3,256,256]{2,1,0:T(8,128)(2,1)}, bf16[3,256,256]{2,1,0:T(8,128)(2,1)S(1)}, u32[]{:S(2)}, u32[]{:S(2)}) collective-permute-start(bf16[3,256,256]{2,1,0:T(8,128)(2,1)} %collective-permute-done.1), channel_id=1, source_target_pairs={{30,0},{99,1},{6,64},{107,65},{14,2},{115,3},{22,66},{123,67},{24,... | collective-permute-start | bytes 1179656 | tf_op jit(solution)/shard_map/ppermute | solution.py:492
  95.0 2.9 %collective-permute-start.11 = (bf16[15,128,256]{2,1,0:T(8,128)(2,1)}, bf16[15,128,256]{2,1,0:T(8,128)(2,1)S(1)}, u32[]{:S(2)}, u32[]{:S(2)}) collective-permute-start(bf16[15,128,256]{2,1,0:T(8,128)(2,1)} %get-tuple-element.29), channel_id=1, source_target_pairs={{0,1},{1,0},{2,3},{3,2},{4,5},{5,4},{6,7},{7,6},{8,9},{9,8},{10,11... | collective-permute-start | bytes 2949128 | tf_op jit(solution)/shard_map/ppermute | solution.py:496
  106.6 64.8 %collective-permute-start.20 = (bf16[8,8,128,128]{3,2,1,0:T(8,128)(2,1)}, bf16[8,8,128,128]{3,2,1,0:T(8,128)(2,1)S(1)}, u32[]{:S(2)}, u32[]{:S(2)}) collective-permute-start(bf16[8,8,128,128]{3,2,1,0:T(8,128)(2,1)} %get-tuple-element.42), channel_id=1, source_target_pairs={{0,8},{2,10},{4,12},{6,14},{8,0},{10,2},{12,4},{14,6},{1,9},{3,11}... | collective-permute-start | bytes 6291464 | tf_op jit(solution)/shard_map/ppermute | solution.py:455
  137.2 25.3 %collective-permute-start.13 = (bf16[4,8,128,128]{3,2,1,0:T(8,128)(2,1)}, bf16[4,8,128,128]{3,2,1,0:T(8,128)(2,1)S(1)}, u32[]{:S(2)}, u32[]{:S(2)}) collective-permute-start(bf16[4,8,128,128]{3,2,1,0:T(8,128)(2,1)} %get-tuple-element.31), channel_id=1, source_target_pairs={{0,2},{2,0},{4,6},{6,4},{8,10},{10,8},{12,14},{14,12},{1,3},{3,1},... | collective-permute-start | bytes 3145736 | tf_op jit(solution)/shard_map/ppermute | solution.py:455
  137.2 26.6 %collective-permute-start.14 = (bf16[4,8,128,128]{3,2,1,0:T(8,128)(2,1)}, bf16[4,8,128,128]{3,2,1,0:T(8,128)(2,1)}, u32[]{:S(2)}, u32[]{:S(2)}) collective-permute-start(bf16[4,8,128,128]{3,2,1,0:T(8,128)(2,1)} %get-tuple-element.33), channel_id=1, source_target_pairs={{0,6},{2,4},{4,2},{6,0},{8,14},{10,12},{12,10},{14,8},{1,7},{3,5},... | collective-permute-start | bytes 3145736 | tf_op jit(solution)/shard_map/ppermute | solution.py:455
  167.3 16.0 %collective-permute-start.15 = (bf16[2,8,128,128]{3,2,1,0:T(8,128)(2,1)}, bf16[2,8,128,128]{3,2,1,0:T(8,128)(2,1)S(1)}, u32[]{:S(2)}, u32[]{:S(2)}) collective-permute-start(bf16[2,8,128,128]{3,2,1,0:T(8,128)(2,1)} %get-tuple-element.35), channel_id=1, source_target_pairs={{0,6},{2,4},{4,2},{6,0},{8,14},{10,12},{12,10},{14,8},{1,7},{3,5},... | collective-permute-start | bytes 1572872 | tf_op jit(solution)/shard_map/ppermute | solution.py:455
  167.6 15.6 %collective-permute-start.16 = (bf16[2,8,128,128]{3,2,1,0:T(8,128)(2,1)}, bf16[2,8,128,128]{3,2,1,0:T(8,128)(2,1)S(1)}, u32[]{:S(2)}, u32[]{:S(2)}) collective-permute-start(bf16[2,8,128,128]{3,2,1,0:T(8,128)(2,1)} %get-tuple-element.36), channel_id=1, source_target_pairs={{0,2},{2,0},{4,6},{6,4},{8,10},{10,8},{12,14},{14,12},{1,3},{3,1},... | collective-permute-start | bytes 1572872 | tf_op jit(solution)/shard_map/ppermute | solution.py:455
  176.2 15.7 %collective-permute-start.21 = (bf16[2,8,128,128]{3,2,1,0:T(8,128)(2,1)}, bf16[2,8,128,128]{3,2,1,0:T(8,128)(2,1)S(1)}, u32[]{:S(2)}, u32[]{:S(2)}) collective-permute-start(bf16[2,8,128,128]{3,2,1,0:T(8,128)(2,1)} %get-tuple-element.45), channel_id=1, source_target_pairs={{0,2},{2,0},{4,6},{6,4},{8,10},{10,8},{12,14},{14,12},{1,3},{3,1},... | collective-permute-start | bytes 1572872 | tf_op jit(solution)/shard_map/ppermute | solution.py:455
  176.3 16.6 %collective-permute-start.22 = (bf16[2,8,128,128]{3,2,1,0:T(8,128)(2,1)}, bf16[2,8,128,128]{3,2,1,0:T(8,128)(2,1)S(1)}, u32[]{:S(2)}, u32[]{:S(2)}) collective-permute-start(bf16[2,8,128,128]{3,2,1,0:T(8,128)(2,1)} %get-tuple-element.46), channel_id=1, source_target_pairs={{0,6},{2,4},{4,2},{6,0},{8,14},{10,12},{12,10},{14,8},{1,7},{3,5},... | collective-permute-start | bytes 1572872 | tf_op jit(solution)/shard_map/ppermute | solution.py:455
  187.3 17.6 %collective-permute-start.17 = (f32[8,128,128]{2,1,0:T(8,128)}, f32[8,128,128]{2,1,0:T(8,128)S(1)}, u32[]{:S(2)}, u32[]{:S(2)}) collective-permute-start(f32[8,128,128]{2,1,0:T(8,128)} %get-tuple-element.38), channel_id=1, source_target_pairs={{0,1},{1,0},{2,3},{3,2},{4,5},{5,4},{6,7},{7,6},{8,9},{9,8},{10,11... | collective-permute-start | bytes 1572872 | tf_op jit(solution)/shard_map/ppermute | solution.py:512
  187.4 12.0 %collective-permute-start.18 = (bf16[8,128,128]{2,1,0:T(8,128)(2,1)}, bf16[8,128,128]{2,1,0:T(8,128)(2,1)S(1)}, u32[]{:S(2)}, u32[]{:S(2)}) collective-permute-start(bf16[8,128,128]{2,1,0:T(8,128)(2,1)} %get-tuple-element.39), channel_id=1, source_target_pairs={{0,8},{1,9},{2,10},{3,11},{4,12},{5,13},{6,14},{7,15},{8,0},{9,1},... | collective-permute-start | bytes 786440 | tf_op jit(solution)/shard_map/ppermute | solution.py:451
  196.7 11.4 %collective-permute-start.23 = (f32[8,128,128]{2,1,0:T(8,128)}, f32[8,128,128]{2,1,0:T(8,128)S(1)}, u32[]{:S(2)}, u32[]{:S(2)}) collective-permute-start(f32[8,128,128]{2,1,0:T(8,128)} %get-tuple-element.48), channel_id=1, source_target_pairs={{0,1},{1,0},{2,3},{3,2},{4,5},{5,4},{6,7},{7,6},{8,9},{9,8},{10,11... | collective-permute-start | bytes 1572872 | tf_op jit(solution)/shard_map/ppermute | solution.py:514
  196.8 8.1 %collective-permute-start.19 = (bf16[8,128,128]{2,1,0:T(8,128)(2,1)S(1)}, bf16[8,128,128]{2,1,0:T(8,128)(2,1)S(1)}, u32[]{:S(2)}, u32[]{:S(2)}) collective-permute-start(bf16[8,128,128]{2,1,0:T(8,128)(2,1)S(1)} %copy-done.24), channel_id=1, source_target_pairs={{0,9},{1,8},{2,11},{3,10},{4,13},{5,12},{6,15},{7,14},{8,1},{9,0},... | collective-permute-start | bytes 786440 | tf_op jit(solution)/shard_map/ppermute | solution.py:451
  197.5 9.2 %collective-permute-start.24 = (bf16[8,128,128]{2,1,0:T(8,128)(2,1)}, bf16[8,128,128]{2,1,0:T(8,128)(2,1)S(1)}, u32[]{:S(2)}, u32[]{:S(2)}) collective-permute-start(bf16[8,128,128]{2,1,0:T(8,128)(2,1)} %get-tuple-element.49), channel_id=1, source_target_pairs={{0,6},{1,3},{2,4},{3,1},{4,2},{5,7},{6,0},{7,5},{8,14},{9,11},{10,... | collective-permute-start | bytes 786440 | tf_op jit(solution)/shard_map/ppermute | solution.py:451
  199.4 8.7 %collective-permute-start.25 = (bf16[8,128,128]{2,1,0:T(8,128)(2,1)}, bf16[8,128,128]{2,1,0:T(8,128)(2,1)S(1)}, u32[]{:S(2)}, u32[]{:S(2)}) collective-permute-start(bf16[8,128,128]{2,1,0:T(8,128)(2,1)} %get-tuple-element.50), channel_id=1, source_target_pairs={{0,3},{1,6},{2,1},{3,4},{4,7},{5,2},{6,5},{7,0},{8,11},{9,14},{10,... | collective-permute-start | bytes 786440 | tf_op jit(solution)/shard_map/ppermute | solution.py:451
  (20 other events, 81.7 us)
where the time goes:
time: 214 us; the launch traced here: 213 us
  waiting for transfers between devices  71.7 us (34%)
  starting transfers between devices  69.1 us (32%)
  Pallas kernels  61.9 us (29%)
  local copies, waits for them, and re-layouts  8.67 us (4%)
    ppermute x7, waiting for transfers between devices, step_y(): return lax.ppermute(value, 'vb', [(j, j ^ bits) for j in range(8)])  41 us
    ppermute x5, starting transfers between devices, program(): mirrors.append(lax.ppermute(mid, AXES, back))  24.7 us
    ppermute x7, starting transfers between devices, step_y(): return lax.ppermute(value, 'vb', [(j, j ^ bits) for j in range(8)])  20.9 us
    pallas_call x2, Pallas kernels, contract(): pl.pallas_call(lambda *refs: contract_kernel(low, *refs), in_specs=[smem,...  19.7 us
    pallas_call x5, Pallas kernels, coulomb(): pl.pallas_call(lambda *refs: coulomb_kernel(start, chunks, *refs), in_spe...  19.3 us
    ppermute x5, starting transfers between devices, program(): mid = lax.ppermute(tile, AXES, out)  18.9 us
    ppermute x5, waiting for transfers between devices, program(): mid = lax.ppermute(tile, AXES, out)  10.1 us
    ppermute x5, waiting for transfers between devices, program(): mirrors.append(lax.ppermute(mid, AXES, back))  8.58 us
  transfers between devices with their start and end apart: 26, of which 16 were waited for; matrix products, arithmetic and copies ran while one was open for 2% of the time, Pallas kernels for 23%

commit v1 on v0

--- a/solution.py
+++ b/solution.py
@@ -115,7 +115,7 @@
             p = chunk * count + row
             gap = base - occ_ref[pair_ref[p, 0]] - occ_ref[pair_ref[p, 1]]
             tile = tiles[chunk][row].astype(jnp.float32)
-            swapped = mirrors[chunk][row].T.astype(jnp.float32)
+            swapped = mirrors[chunk][row].astype(jnp.float32).T
             work_ref[p % 2] = ((2.0 * tile - swapped) / gap).astype(jnp.bfloat16)
             keep_ref[p] = work_ref[p % 2, pl.ds(mine, half), :]
             send_ref[p] = work_ref[p % 2, pl.ds(other, half), :]
@@ -377,17 +377,18 @@
     blocks = PER_OWNER // 2
     half = kept_buf.shape[-2]
     loads = []
-    for part in range(2):
-        for side in range(2):
-            at = 2 * part + side
+    for block in range(blocks):
+        rows = slice(block * SPLIT, (block + 1) * SPLIT)
+        for at in range(4):
+            kept, far = ins[at // 2 * 4 + at % 2], ins[at // 2 * 4 + 2 + at % 2]
             loads += [
-                pltpu.make_async_copy(ins[4 * part + side], kept_buf.at[at], in_sems.at[0, at]),
-                pltpu.make_async_copy(ins[4 * part + 2 + side], far_buf.at[at], in_sems.at[1, at]),
+                pltpu.make_async_copy(
+                    kept.at[rows], kept_buf.at[at, rows], in_sems.at[0, at, block]
+                ),
+                pltpu.make_async_copy(far.at[rows], far_buf.at[at, rows], in_sems.at[1, at, block]),
             ]
     for copy in loads:
         copy.start()
-    for copy in loads:
-        copy.wait()
 
     def write(block, order):
         rows = slice(block * BLOCK, (block + 1) * BLOCK)
@@ -401,6 +402,8 @@
 
     stores = []
     for block in range(blocks):
+        for copy in loads[block * 8 : (block + 1) * 8]:
+            copy.wait()
 
         @pl.when(core == 0)
         def _():
@@ -432,7 +435,7 @@
             pltpu.VMEM((4, group, half, width), jnp.float32),
             pltpu.VMEM((4, group, half, width), jnp.bfloat16),
             pltpu.VMEM(shape.shape, jnp.float32),
-            pltpu.SemaphoreType.DMA((2, 4)),
+            pltpu.SemaphoreType.DMA((2, 4, blocks)),
             pltpu.SemaphoreType.DMA((blocks,)),
         ],
         cost_estimate=pl.CostEstimate(

time: 214 us -> 214 us (level)
  no operation moved by 1% of the time
where the time goes in v1:
time: 214 us; the launch traced here: 213 us
  waiting for transfers between devices  71.7 us (34%)
  starting transfers between devices  69.1 us (32%)
  Pallas kernels  61.7 us (29%)
  local copies, waits for them, and re-layouts  8.67 us (4%)
    ppermute x7, waiting for transfers between devices, step_y(): return lax.ppermute(value, 'vb', [(j, j ^ bits) for j in range(8)])  41 us
    ppermute x5, starting transfers between devices, program(): mirrors.append(lax.ppermute(mid, AXES, back))  24.7 us
    ppermute x7, starting transfers between devices, step_y(): return lax.ppermute(value, 'vb', [(j, j ^ bits) for j in range(8)])  20.9 us
    pallas_call x2, Pallas kernels, contract(): pl.pallas_call(lambda *refs: contract_kernel(low, *refs), in_specs=[smem,...  19.7 us
    pallas_call x5, Pallas kernels, coulomb(): pl.pallas_call(lambda *refs: coulomb_kernel(start, chunks, *refs), in_spe...  19.3 us
    ppermute x5, starting transfers between devices, program(): mid = lax.ppermute(tile, AXES, out)  18.9 us
    ppermute x5, waiting for transfers between devices, program(): mid = lax.ppermute(tile, AXES, out)  10.1 us
    ppermute x5, waiting for transfers between devices, program(): mirrors.append(lax.ppermute(mid, AXES, back))  8.58 us
  transfers between devices with their start and end apart: 26, of which 16 were waited for; matrix products, arithmetic and copies ran while one was open for 2% of the time, Pallas kernels for 23%

profile of v1, /device:TPU:0, one launch (start us, length us, event | category | flops | bytes accessed | tf_op | source)
XLA Modules:
  0.0 213.2 jit_solution(7801011030250082655)
XLA Ops:
  0.0 3.8 %coulomb.5.refs_2_.refs_8_ = bf16[3,256,256]{2,1,0:T(8,128)(2,1)} custom-call(bf16[15,256,1536]{2,1,0:T(8,128)(2,1)} %refs_0_.9, bf16[15,256,1536]{2,1,0:T(8,128)(2,1)} %refs_4_.3), custom_call_target="tpu_custom_call" | custom-call | flops 603979776 | bytes 5111808 | tf_op jit(solution)/shard_map/coulomb/pallas_call | solution.py:68
  3.9 3.9 %coulomb.6.refs_2_.refs_9_ = bf16[3,256,256]{2,1,0:T(8,128)(2,1)} custom-call(bf16[15,256,1536]{2,1,0:T(8,128)(2,1)} %refs_0_.9, bf16[15,256,1536]{2,1,0:T(8,128)(2,1)} %refs_4_.3, bf16[3,256,256]{2,1,0:T(8,128)(2,1)} %coulomb.5.refs_2_.refs_8_), custom_call_target="tpu_custom_call" | custom-call | flops 603979776 | bytes 5111808 | tf_op jit(solution)/shard_map/coulomb/pallas_call | solution.py:68
  7.7 3.8 %coulomb.7.refs_2_.refs_10_ = bf16[3,256,256]{2,1,0:T(8,128)(2,1)} custom-call(bf16[15,256,1536]{2,1,0:T(8,128)(2,1)} %refs_0_.9, bf16[15,256,1536]{2,1,0:T(8,128)(2,1)} %refs_4_.3, bf16[3,256,256]{2,1,0:T(8,128)(2,1)} %coulomb.6.refs_2_.refs_9_), custom_call_target="tpu_custom_call" | custom-call | flops 603979776 | bytes 5111808 | tf_op jit(solution)/shard_map/coulomb/pallas_call | solution.py:68
  11.5 3.8 %coulomb.8.refs_2_.refs_11_ = bf16[3,256,256]{2,1,0:T(8,128)(2,1)} custom-call(bf16[15,256,1536]{2,1,0:T(8,128)(2,1)} %refs_0_.9, bf16[15,256,1536]{2,1,0:T(8,128)(2,1)} %refs_4_.3, bf16[3,256,256]{2,1,0:T(8,128)(2,1)} %coulomb.7.refs_2_.refs_10_), custom_call_target="tpu_custom_call" | custom-call | flops 603979776 | bytes 5111808 | tf_op jit(solution)/shard_map/coulomb/pallas_call | solution.py:68
  15.5 3.9 %coulomb.9.refs_12_ = bf16[3,256,256]{2,1,0:T(8,128)(2,1)} custom-call(bf16[15,256,1536]{2,1,0:T(8,128)(2,1)} %refs_0_.9, bf16[15,256,1536]{2,1,0:T(8,128)(2,1)} %refs_4_.3, bf16[3,256,256]{2,1,0:T(8,128)(2,1)} %coulomb.8.refs_2_.refs_11_), custom_call_target="tpu_custom_call" | custom-call | flops 603979776 | bytes 5111808 | tf_op jit(solution)/shard_map/coulomb/pallas_call | solution.py:68
  19.4 4.7 %collective-permute-start.9 = (bf16[3,256,256]{2,1,0:T(8,128)(2,1)}, bf16[3,256,256]{2,1,0:T(8,128)(2,1)}, u32[]{:S(2)}, u32[]{:S(2)}) collective-permute-start(bf16[3,256,256]{2,1,0:T(8,128)(2,1)} %coulomb.9.refs_12_), channel_id=1, source_target_pairs={{0,12},{1,57},{8,20},{9,33},{16,28},{17,41},{24,4},{25,49},{2,14},... | collective-permute-start | bytes 1179656 | tf_op jit(solution)/shard_map/ppermute | solution.py:494
  24.1 4.1 %collective-permute-start.7 = (bf16[3,256,256]{2,1,0:T(8,128)(2,1)S(1)}, bf16[3,256,256]{2,1,0:T(8,128)(2,1)S(1)}, u32[]{:S(2)}, u32[]{:S(2)}) collective-permute-start(bf16[3,256,256]{2,1,0:T(8,128)(2,1)S(1)} %copy-done.5), channel_id=1, source_target_pairs={{0,104},{1,69},{8,112},{9,77},{16,120},{17,85},{24,96},{25,93},{2,... | collective-permute-start | bytes 1179656 | tf_op jit(solution)/shard_map/ppermute | solution.py:494
  30.9 1.7 collective-permute-start.3
  33.9 8.2 %collective-permute-start.1 = (bf16[3,256,256]{2,1,0:T(8,128)(2,1)S(1)}, bf16[3,256,256]{2,1,0:T(8,128)(2,1)}, u32[]{:S(2)}, u32[]{:S(2)}) collective-permute-start(bf16[3,256,256]{2,1,0:T(8,128)(2,1)S(1)} %copy-done.2), channel_id=1, source_target_pairs={{0,30},{1,99},{8,6},{9,107},{16,14},{17,115},{24,22},{25,123},{2,2... | collective-permute-start | bytes 1179656 | tf_op jit(solution)/shard_map/ppermute | solution.py:494
  43.7 6.2 %collective-permute-done.5 = bf16[3,256,256]{2,1,0:T(8,128)(2,1)S(1)} collective-permute-done((bf16[3,256,256]{2,1,0:T(8,128)(2,1)S(1)}, bf16[3,256,256]{2,1,0:T(8,128)(2,1)S(1)}, u32[]{:S(2)}, u32[]{:S(2)}) %collective-permute-start.5) | collective-permute-done | bytes 393248 | tf_op jit(solution)/shard_map/ppermute | solution.py:494
  50.0 10.4 %collective-permute-start.8 = (bf16[3,256,256]{2,1,0:T(8,128)(2,1)S(1)}, bf16[3,256,256]{2,1,0:T(8,128)(2,1)S(1)}, u32[]{:S(2)}, u32[]{:S(2)}) collective-permute-start(bf16[3,256,256]{2,1,0:T(8,128)(2,1)S(1)} %collective-permute-done.7), channel_id=1, source_target_pairs={{104,0},{69,1},{112,64},{77,65},{120,2},{85,3},{96,66},{93,67},{10... | collective-permute-start | bytes 1179656 | tf_op jit(solution)/shard_map/ppermute | solution.py:495
  60.4 2.6 %collective-permute-done.1 = bf16[3,256,256]{2,1,0:T(8,128)(2,1)} collective-permute-done((bf16[3,256,256]{2,1,0:T(8,128)(2,1)S(1)}, bf16[3,256,256]{2,1,0:T(8,128)(2,1)}, u32[]{:S(2)}, u32[]{:S(2)}) %collective-permute-start.1) | collective-permute-done | bytes 393248 | tf_op jit(solution)/shard_map/ppermute | solution.py:494
  62.9 10.0 %collective-permute-start.4 = (bf16[3,256,256]{2,1,0:T(8,128)(2,1)S(1)}, bf16[3,256,256]{2,1,0:T(8,128)(2,1)S(1)}, u32[]{:S(2)}, u32[]{:S(2)}) collective-permute-start(bf16[3,256,256]{2,1,0:T(8,128)(2,1)S(1)} %collective-permute-done.3), channel_id=1, source_target_pairs={{38,0},{11,1},{46,64},{19,65},{54,2},{27,3},{62,66},{3,67},{32,16}... | collective-permute-start | bytes 1179656 | tf_op jit(solution)/shard_map/ppermute | solution.py:495
  73.0 2.6 %collective-permute-start.2 = (bf16[3,256,256]{2,1,0:T(8,128)(2,1)}, bf16[3,256,256]{2,1,0:T(8,128)(2,1)S(1)}, u32[]{:S(2)}, u32[]{:S(2)}) collective-permute-start(bf16[3,256,256]{2,1,0:T(8,128)(2,1)} %collective-permute-done.1), channel_id=1, source_target_pairs={{30,0},{99,1},{6,64},{107,65},{14,2},{115,3},{22,66},{123,67},{24,... | collective-permute-start | bytes 1179656 | tf_op jit(solution)/shard_map/ppermute | solution.py:495
  81.0 7.5 %collective-permute-done.2.refs_13_ = bf16[3,256,256]{2,1,0:T(8,128)(2,1)S(1)} collective-permute-done((bf16[3,256,256]{2,1,0:T(8,128)(2,1)}, bf16[3,256,256]{2,1,0:T(8,128)(2,1)S(1)}, u32[]{:S(2)}, u32[]{:S(2)}) %collective-permute-start.2) | collective-permute-done | bytes 393248 | tf_op jit(solution)/shard_map/ppermute | solution.py:495
  89.3 5.9 %amplitude.1 = (bf16[15,128,256]{2,1,0:T(8,128)(2,1)}, bf16[15,128,256]{2,1,0:T(8,128)(2,1)}) custom-call(s32[1]{0:T(128)} %bitcast.refs_0_.core_ref, f32[8]{0:T(128)} %refs_1_.11, s32[15,2]{1,0:T(8,128)} %copy.10.refs_2_, s32[2,15,12]{2,1,0:T(8,128)} %get-tuple-element.51.refs_3_.refs_0_, s32[2,15,12]{2,1,0:T(8,128)} %get-tuple-element.52.refs_4_.refs_0_, ...), custom_call_target="tpu_custom_call" | custom-call | flops 9830400 | bytes 5898240 | tf_op jit(solution)/shard_map/amplitude/pallas_call | solution.py:132
  95.3 2.8 %collective-permute-done.11.refs_3_ = bf16[15,128,256]{2,1,0:T(8,128)(2,1)S(1)} collective-permute-done((bf16[15,128,256]{2,1,0:T(8,128)(2,1)}, bf16[15,128,256]{2,1,0:T(8,128)(2,1)S(1)}, u32[]{:S(2)}, u32[]{:S(2)}) %collective-permute-start.11) | collective-permute-done | bytes 983072 | tf_op jit(solution)/shard_map/ppermute | solution.py:499
  99.0 7.8 %contract.3 = (bf16[4,8,128,128]{3,2,1,0:T(8,128)(2,1)}, bf16[4,8,128,128]{3,2,1,0:T(8,128)(2,1)}, bf16[8,8,128,128]{3,2,1,0:T(8,128)(2,1)}) custom-call(s32[2,15,12]{2,1,0:T(8,128)} %get-tuple-element.51.refs_3_.refs_0_, s32[2,15]{1,0:T(2,128)} %fusion.2.refs_5_.refs_1_, bf16[15,128,256]{2,1,0:T(8,128)(2,1)} %get-tuple-element.28.refs_2_, ...), custom_call_target="tpu_custom_call" | custom-call | flops 1509949440 | bytes 15990784 | tf_op jit(solution)/shard_map/contract/pallas_call | solution.py:211
  106.8 18.6 %collective-permute-start.20 = (bf16[8,8,128,128]{3,2,1,0:T(8,128)(2,1)}, bf16[8,8,128,128]{3,2,1,0:T(8,128)(2,1)S(1)}, u32[]{:S(2)}, u32[]{:S(2)}) collective-permute-start(bf16[8,8,128,128]{3,2,1,0:T(8,128)(2,1)} %get-tuple-element.42), channel_id=1, source_target_pairs={{0,8},{2,10},{4,12},{6,14},{8,0},{10,2},{12,4},{14,6},{1,9},{3,11}... | collective-permute-start | bytes 6291464 | tf_op jit(solution)/shard_map/ppermute | solution.py:458
  125.4 11.9 %contract.2 = (bf16[4,8,128,128]{3,2,1,0:T(8,128)(2,1)}, bf16[4,8,128,128]{3,2,1,0:T(8,128)(2,1)}, bf16[4,8,128,128]{3,2,1,0:T(8,128)(2,1)}, bf16[4,8,128,128]{3,2,1,0:T(8,128)(2,1)}) custom-call(s32[2,15,12]{2,1,0:T(8,128)} %get-tuple-element.52.refs_4_.refs_0_, s32[2,15]{1,0:T(2,128)} %fusion.2.refs_5_.refs_1_, ...), custom_call_target="tpu_custom_call" | custom-call | flops 1509949440 | bytes 15990784 | tf_op jit(solution)/shard_map/contract/pallas_call | solution.py:211
  137.5 25.1 %collective-permute-done.13.refs_1_ = bf16[4,8,128,128]{3,2,1,0:T(8,128)(2,1)S(1)} collective-permute-done((bf16[4,8,128,128]{3,2,1,0:T(8,128)(2,1)}, bf16[4,8,128,128]{3,2,1,0:T(8,128)(2,1)S(1)}, u32[]{:S(2)}, u32[]{:S(2)}) %collective-permute-start.13) | collective-permute-done | bytes 1048608 | tf_op jit(solution)/shard_map/ppermute | solution.py:458
  164.0 3.4 %add_halves.2 = (f32[2,2,8,128,128]{4,3,2,1,0:T(8,128)}, bf16[2,8,128,128]{3,2,1,0:T(8,128)(2,1)}, bf16[2,8,128,128]{3,2,1,0:T(8,128)(2,1)}) custom-call(bf16[4,8,128,128]{3,2,1,0:T(8,128)(2,1)} %get-tuple-element.30.refs_0_, bf16[4,8,128,128]{3,2,1,0:T(8,128)(2,1)} %copy-done.6, bf16[4,8,128,128]{3,2,1,0:T(8,128)(2,1)} %get-tuple-element.32.refs_2_, ...), custom_call_target="tpu_custom_call" | custom-call | flops 1048576 | bytes 7340032 | tf_op jit(solution)/shard_map/add_halves/pallas_call | solution.py:284
  168.2 3.4 %collective-permute-done.20.refs_1_.refs_3_ = bf16[8,8,128,128]{3,2,1,0:T(8,128)(2,1)S(1)} collective-permute-done((bf16[8,8,128,128]{3,2,1,0:T(8,128)(2,1)}, bf16[8,8,128,128]{3,2,1,0:T(8,128)(2,1)S(1)}, u32[]{:S(2)}, u32[]{:S(2)}) %collective-permute-start.20) | collective-permute-done | bytes 2097184 | tf_op jit(solution)/shard_map/ppermute | solution.py:458
  173.0 3.4 %add_halves.3 = (f32[2,2,8,128,128]{4,3,2,1,0:T(8,128)}, bf16[2,8,128,128]{3,2,1,0:T(8,128)(2,1)}, bf16[2,8,128,128]{3,2,1,0:T(8,128)(2,1)}) custom-call(bf16[4,8,128,128]{3,2,1,0:T(8,128)(2,1)} %get-tuple-element.41.refs_0_, bf16[8,8,128,128]{3,2,1,0:T(8,128)(2,1)} %copy-done, bf16[4,8,128,128]{3,2,1,0:T(8,128)(2,1)} %get-tuple-element.43.refs_2_, ...), custom_call_target="tpu_custom_call" | custom-call | flops 1048576 | bytes 7340032 | tf_op jit(solution)/shard_map/add_halves/pallas_call | solution.py:284
  177.7 5.8 %collective-permute-done.15.other0 = bf16[2,8,128,128]{3,2,1,0:T(8,128)(2,1)S(1)} collective-permute-done((bf16[2,8,128,128]{3,2,1,0:T(8,128)(2,1)}, bf16[2,8,128,128]{3,2,1,0:T(8,128)(2,1)S(1)}, u32[]{:S(2)}, u32[]{:S(2)}) %collective-permute-start.15) | collective-permute-done | bytes 524320 | tf_op jit(solution)/shard_map/ppermute | solution.py:458
  184.4 3.1 %last_add.2 = (f32[8,128,128]{2,1,0:T(8,128)}, f32[8,128,128]{2,1,0:T(8,128)}, bf16[8,128,128]{2,1,0:T(8,128)(2,1)}, bf16[8,128,128]{2,1,0:T(8,128)(2,1)}) custom-call(s32[1]{0:T(128)} %bitcast.refs_0_.core_ref, f32[2,2,8,128,128]{4,3,2,1,0:T(8,128)} %get-tuple-element.34.kept_in, bf16[2,8,128,128]{3,2,1,0:T(8,128)(2,1)} %copy-done.9, ...), custom_call_target="tpu_custom_call" | custom-call | flops 524288 | bytes 5242880 | tf_op jit(solution)/shard_map/last_add/pallas_call | solution.py:353
  187.7 4.4 %collective-permute-done.21.other0 = bf16[2,8,128,128]{3,2,1,0:T(8,128)(2,1)S(1)} collective-permute-done((bf16[2,8,128,128]{3,2,1,0:T(8,128)(2,1)}, bf16[2,8,128,128]{3,2,1,0:T(8,128)(2,1)S(1)}, u32[]{:S(2)}, u32[]{:S(2)}) %collective-permute-start.21) | collective-permute-done | bytes 524320 | tf_op jit(solution)/shard_map/ppermute | solution.py:458
  193.8 3.1 %last_add.3 = (f32[8,128,128]{2,1,0:T(8,128)}, f32[8,128,128]{2,1,0:T(8,128)}, bf16[8,128,128]{2,1,0:T(8,128)(2,1)}, bf16[8,128,128]{2,1,0:T(8,128)(2,1)}) custom-call(s32[1]{0:T(128)} %bitcast.refs_0_.core_ref, f32[2,2,8,128,128]{4,3,2,1,0:T(8,128)} %get-tuple-element.44.kept_in, bf16[2,8,128,128]{3,2,1,0:T(8,128)(2,1)} %copy-done.7, ...), custom_call_target="tpu_custom_call" | custom-call | flops 524288 | bytes 5242880 | tf_op jit(solution)/shard_map/last_add/pallas_call | solution.py:353
  197.7 1.9 collective-permute-start.24
  199.6 5.5 %collective-permute-done.19.refs_3_ = bf16[8,128,128]{2,1,0:T(8,128)(2,1)S(1)} collective-permute-done((bf16[8,128,128]{2,1,0:T(8,128)(2,1)S(1)}, bf16[8,128,128]{2,1,0:T(8,128)(2,1)S(1)}, u32[]{:S(2)}, u32[]{:S(2)}) %collective-permute-start.19) | collective-permute-done | bytes 262176 | tf_op jit(solution)/shard_map/ppermute | solution.py:454
  205.1 1.8 collective-permute-done.24.refs_6_
  209.2 3.8 %finish.1 = f32[256,8,256]{2,1,0:T(8,128)} custom-call(s32[1]{0:T(128)} %bitcast.refs_0_.core_ref, f32[8,128,128]{2,1,0:T(8,128)} %get-tuple-element.37.refs_0_, f32[8,128,128]{2,1,0:T(8,128)} %copy-done.11, bf16[8,128,128]{2,1,0:T(8,128)(2,1)} %copy-done.18, bf16[8,128,128]{2,1,0:T(8,128)(2,1)} %copy-done.19, f32[8,128,128]{2,1,0:T(8,128)} %get-tuple-element.47.refs_4_, ...), custom_call_target="tpu_custom_call" | custom-call | flops 524288 | bytes 5242880 | tf_op jit(solution)/shard_map/finish/pallas_call | solution.py:429
  (93 shorter events, 23.6 us)
Async XLA Ops:
  0.0 98.0 %collective-permute-start.12 = (bf16[15,256,1536]{2,1,0:T(8,128)(2,1)}, bf16[15,256,1536]{2,1,0:T(8,128)(2,1)}, u32[]{:S(2)}, u32[]{:S(2)}) collective-permute-start(bf16[15,256,1536]{2,1,0:T(8,128)(2,1)} %refs_4_.3), channel_id=1, source_target_pairs={{0,1},{1,0},{2,3},{3,2},{4,5},{5,4},{6,7},{7,6},{8,9},{9,8},{10,11... | collective-permute-start | bytes 35389448 | tf_op jit(solution)/shard_map/ppermute | solution.py:486
  15.4 12.9 %copy-start.22 = (s32[15,12]{1,0:T(8,128)S(1)}, s32[15,12]{1,0:T(8,128)}, u32[]{:S(2)}) copy-start(s32[15,12]{1,0:T(8,128)} %param.11) | copy-start | bytes 2164
  15.4 14.6 %copy-start.4 = (bf16[3,256,256]{2,1,0:T(8,128)(2,1)S(1)}, bf16[3,256,256]{2,1,0:T(8,128)(2,1)}, u32[]{:S(2)}) copy-start(bf16[3,256,256]{2,1,0:T(8,128)(2,1)} %coulomb.7.refs_2_.refs_10_) | copy-start | bytes 1179652
  15.4 15.4 %copy-start.3 = (bf16[3,256,256]{2,1,0:T(8,128)(2,1)S(1)}, bf16[3,256,256]{2,1,0:T(8,128)(2,1)}, u32[]{:S(2)}) copy-start(bf16[3,256,256]{2,1,0:T(8,128)(2,1)} %coulomb.6.refs_2_.refs_9_) | copy-start | bytes 1179652
  15.4 18.4 %copy-start.2 = (bf16[3,256,256]{2,1,0:T(8,128)(2,1)S(1)}, bf16[3,256,256]{2,1,0:T(8,128)(2,1)}, u32[]{:S(2)}) copy-start(bf16[3,256,256]{2,1,0:T(8,128)(2,1)} %coulomb.5.refs_2_.refs_8_) | copy-start | bytes 1179652
  15.4 60.1 %copy-start.23 = (s32[15,2]{0,1:T(2,128)S(1)}, s32[15,2]{0,1:T(2,128)}, u32[]{:S(2)}) copy-start(s32[15,2]{0,1:T(2,128)} %param.10) | copy-start | bytes 364
  19.4 14.5 %collective-permute-start.9 = (bf16[3,256,256]{2,1,0:T(8,128)(2,1)}, bf16[3,256,256]{2,1,0:T(8,128)(2,1)}, u32[]{:S(2)}, u32[]{:S(2)}) collective-permute-start(bf16[3,256,256]{2,1,0:T(8,128)(2,1)} %coulomb.9.refs_12_), channel_id=1, source_target_pairs={{0,12},{1,57},{8,20},{9,33},{16,28},{17,41},{24,4},{25,49},{2,14},... | collective-permute-start | bytes 1179656 | tf_op jit(solution)/shard_map/ppermute | solution.py:494
  24.1 18.0 %collective-permute-start.7 = (bf16[3,256,256]{2,1,0:T(8,128)(2,1)S(1)}, bf16[3,256,256]{2,1,0:T(8,128)(2,1)S(1)}, u32[]{:S(2)}, u32[]{:S(2)}) collective-permute-start(bf16[3,256,256]{2,1,0:T(8,128)(2,1)S(1)} %copy-done.5), channel_id=1, source_target_pairs={{0,104},{1,69},{8,112},{9,77},{16,120},{17,85},{24,96},{25,93},{2,... | collective-permute-start | bytes 1179656 | tf_op jit(solution)/shard_map/ppermute | solution.py:494
  28.4 2.5 %collective-permute-start = (s32[15,13]{1,0:T(8,128)S(1)}, s32[15,13]{1,0:T(8,128)S(1)}, u32[]{:S(2)}, u32[]{:S(2)}) collective-permute-start(s32[15,13]{1,0:T(8,128)S(1)} %pad_add_fusion.1), channel_id=1, source_target_pairs={{0,1},{1,0},{2,3},{3,2},{4,5},{5,4},{6,7},{7,6},{8,9},{9,8},{10,11... | collective-permute-start | bytes 2348 | tf_op jit(solution)/shard_map/ppermute | solution.py:474
  30.0 19.9 %collective-permute-start.5 = (bf16[3,256,256]{2,1,0:T(8,128)(2,1)S(1)}, bf16[3,256,256]{2,1,0:T(8,128)(2,1)S(1)}, u32[]{:S(2)}, u32[]{:S(2)}) collective-permute-start(bf16[3,256,256]{2,1,0:T(8,128)(2,1)S(1)} %copy-done.4), channel_id=1, source_target_pairs={{0,28},{1,49},{8,4},{9,57},{16,12},{17,33},{24,20},{25,41},{2,30},... | collective-permute-start | bytes 1179656 | tf_op jit(solution)/shard_map/ppermute | solution.py:494
  30.9 29.5 %collective-permute-start.3 = (bf16[3,256,256]{2,1,0:T(8,128)(2,1)S(1)}, bf16[3,256,256]{2,1,0:T(8,128)(2,1)S(1)}, u32[]{:S(2)}, u32[]{:S(2)}) collective-permute-start(bf16[3,256,256]{2,1,0:T(8,128)(2,1)S(1)} %copy-done.3), channel_id=1, source_target_pairs={{0,38},{1,11},{8,46},{9,19},{16,54},{17,27},{24,62},{25,3},{2,32},... | collective-permute-start | bytes 1179656 | tf_op jit(solution)/shard_map/ppermute | solution.py:494
  33.9 29.0 %collective-permute-start.1 = (bf16[3,256,256]{2,1,0:T(8,128)(2,1)S(1)}, bf16[3,256,256]{2,1,0:T(8,128)(2,1)}, u32[]{:S(2)}, u32[]{:S(2)}) collective-permute-start(bf16[3,256,256]{2,1,0:T(8,128)(2,1)S(1)} %copy-done.2), channel_id=1, source_target_pairs={{0,30},{1,99},{8,6},{9,107},{16,14},{17,115},{24,22},{25,123},{2,2... | collective-permute-start | bytes 1179656 | tf_op jit(solution)/shard_map/ppermute | solution.py:494
  42.1 30.9 %collective-permute-start.10 = (bf16[3,256,256]{2,1,0:T(8,128)(2,1)}, bf16[3,256,256]{2,1,0:T(8,128)(2,1)S(1)}, u32[]{:S(2)}, u32[]{:S(2)}) collective-permute-start(bf16[3,256,256]{2,1,0:T(8,128)(2,1)} %collective-permute-done.9), channel_id=1, source_target_pairs={{12,0},{57,1},{20,64},{33,65},{28,2},{41,3},{4,66},{49,67},{14,16}... | collective-permute-start | bytes 1179656 | tf_op jit(solution)/shard_map/ppermute | solution.py:495
  50.0 30.0 %collective-permute-start.8 = (bf16[3,256,256]{2,1,0:T(8,128)(2,1)S(1)}, bf16[3,256,256]{2,1,0:T(8,128)(2,1)S(1)}, u32[]{:S(2)}, u32[]{:S(2)}) collective-permute-start(bf16[3,256,256]{2,1,0:T(8,128)(2,1)S(1)} %collective-permute-done.7), channel_id=1, source_target_pairs={{104,0},{69,1},{112,64},{77,65},{120,2},{85,3},{96,66},{93,67},{10... | collective-permute-start | bytes 1179656 | tf_op jit(solution)/shard_map/ppermute | solution.py:495
  60.4 19.6 %collective-permute-start.6 = (bf16[3,256,256]{2,1,0:T(8,128)(2,1)S(1)}, bf16[3,256,256]{2,1,0:T(8,128)(2,1)S(1)}, u32[]{:S(2)}, u32[]{:S(2)}) collective-permute-start(bf16[3,256,256]{2,1,0:T(8,128)(2,1)S(1)} %collective-permute-done.5), channel_id=1, source_target_pairs={{28,0},{49,1},{4,64},{57,65},{12,2},{33,3},{20,66},{41,67},{30,16}... | collective-permute-start | bytes 1179656 | tf_op jit(solution)/shard_map/ppermute | solution.py:495
  62.9 18.1 %collective-permute-start.4 = (bf16[3,256,256]{2,1,0:T(8,128)(2,1)S(1)}, bf16[3,256,256]{2,1,0:T(8,128)(2,1)S(1)}, u32[]{:S(2)}, u32[]{:S(2)}) collective-permute-start(bf16[3,256,256]{2,1,0:T(8,128)(2,1)S(1)} %collective-permute-done.3), channel_id=1, source_target_pairs={{38,0},{11,1},{46,64},{19,65},{54,2},{27,3},{62,66},{3,67},{32,16}... | collective-permute-start | bytes 1179656 | tf_op jit(solution)/shard_map/ppermute | solution.py:495
  73.0 15.6 %copy-start.13 = (bf16[3,256,256]{2,1,0:T(8,128)(2,1)}, bf16[3,256,256]{2,1,0:T(8,128)(2,1)S(1)}, u32[]{:S(2)}) copy-start(bf16[3,256,256]{2,1,0:T(8,128)(2,1)S(1)} %collective-permute-done.10.refs_17_) | copy-start | bytes 1179652
  73.0 15.5 %collective-permute-start.2 = (bf16[3,256,256]{2,1,0:T(8,128)(2,1)}, bf16[3,256,256]{2,1,0:T(8,128)(2,1)S(1)}, u32[]{:S(2)}, u32[]{:S(2)}) collective-permute-start(bf16[3,256,256]{2,1,0:T(8,128)(2,1)} %collective-permute-done.1), channel_id=1, source_target_pairs={{30,0},{99,1},{6,64},{107,65},{14,2},{115,3},{22,66},{123,67},{24,... | collective-permute-start | bytes 1179656 | tf_op jit(solution)/shard_map/ppermute | solution.py:495
  95.2 2.9 %collective-permute-start.11 = (bf16[15,128,256]{2,1,0:T(8,128)(2,1)}, bf16[15,128,256]{2,1,0:T(8,128)(2,1)S(1)}, u32[]{:S(2)}, u32[]{:S(2)}) collective-permute-start(bf16[15,128,256]{2,1,0:T(8,128)(2,1)} %get-tuple-element.29), channel_id=1, source_target_pairs={{0,1},{1,0},{2,3},{3,2},{4,5},{5,4},{6,7},{7,6},{8,9},{9,8},{10,11... | collective-permute-start | bytes 2949128 | tf_op jit(solution)/shard_map/ppermute | solution.py:499
  106.8 64.8 %collective-permute-start.20 = (bf16[8,8,128,128]{3,2,1,0:T(8,128)(2,1)}, bf16[8,8,128,128]{3,2,1,0:T(8,128)(2,1)S(1)}, u32[]{:S(2)}, u32[]{:S(2)}) collective-permute-start(bf16[8,8,128,128]{3,2,1,0:T(8,128)(2,1)} %get-tuple-element.42), channel_id=1, source_target_pairs={{0,8},{2,10},{4,12},{6,14},{8,0},{10,2},{12,4},{14,6},{1,9},{3,11}... | collective-permute-start | bytes 6291464 | tf_op jit(solution)/shard_map/ppermute | solution.py:458
  137.3 25.3 %collective-permute-start.13 = (bf16[4,8,128,128]{3,2,1,0:T(8,128)(2,1)}, bf16[4,8,128,128]{3,2,1,0:T(8,128)(2,1)S(1)}, u32[]{:S(2)}, u32[]{:S(2)}) collective-permute-start(bf16[4,8,128,128]{3,2,1,0:T(8,128)(2,1)} %get-tuple-element.31), channel_id=1, source_target_pairs={{0,2},{2,0},{4,6},{6,4},{8,10},{10,8},{12,14},{14,12},{1,3},{3,1},... | collective-permute-start | bytes 3145736 | tf_op jit(solution)/shard_map/ppermute | solution.py:458
  137.4 26.6 %collective-permute-start.14 = (bf16[4,8,128,128]{3,2,1,0:T(8,128)(2,1)}, bf16[4,8,128,128]{3,2,1,0:T(8,128)(2,1)}, u32[]{:S(2)}, u32[]{:S(2)}) collective-permute-start(bf16[4,8,128,128]{3,2,1,0:T(8,128)(2,1)} %get-tuple-element.33), channel_id=1, source_target_pairs={{0,6},{2,4},{4,2},{6,0},{8,14},{10,12},{12,10},{14,8},{1,7},{3,5},... | collective-permute-start | bytes 3145736 | tf_op jit(solution)/shard_map/ppermute | solution.py:458
  167.4 16.0 %collective-permute-start.15 = (bf16[2,8,128,128]{3,2,1,0:T(8,128)(2,1)}, bf16[2,8,128,128]{3,2,1,0:T(8,128)(2,1)S(1)}, u32[]{:S(2)}, u32[]{:S(2)}) collective-permute-start(bf16[2,8,128,128]{3,2,1,0:T(8,128)(2,1)} %get-tuple-element.35), channel_id=1, source_target_pairs={{0,6},{2,4},{4,2},{6,0},{8,14},{10,12},{12,10},{14,8},{1,7},{3,5},... | collective-permute-start | bytes 1572872 | tf_op jit(solution)/shard_map/ppermute | solution.py:458
  167.8 15.6 %collective-permute-start.16 = (bf16[2,8,128,128]{3,2,1,0:T(8,128)(2,1)}, bf16[2,8,128,128]{3,2,1,0:T(8,128)(2,1)S(1)}, u32[]{:S(2)}, u32[]{:S(2)}) collective-permute-start(bf16[2,8,128,128]{3,2,1,0:T(8,128)(2,1)} %get-tuple-element.36), channel_id=1, source_target_pairs={{0,2},{2,0},{4,6},{6,4},{8,10},{10,8},{12,14},{14,12},{1,3},{3,1},... | collective-permute-start | bytes 1572872 | tf_op jit(solution)/shard_map/ppermute | solution.py:458
  176.4 15.7 %collective-permute-start.21 = (bf16[2,8,128,128]{3,2,1,0:T(8,128)(2,1)}, bf16[2,8,128,128]{3,2,1,0:T(8,128)(2,1)S(1)}, u32[]{:S(2)}, u32[]{:S(2)}) collective-permute-start(bf16[2,8,128,128]{3,2,1,0:T(8,128)(2,1)} %get-tuple-element.45), channel_id=1, source_target_pairs={{0,2},{2,0},{4,6},{6,4},{8,10},{10,8},{12,14},{14,12},{1,3},{3,1},... | collective-permute-start | bytes 1572872 | tf_op jit(solution)/shard_map/ppermute | solution.py:458
  176.5 16.6 %collective-permute-start.22 = (bf16[2,8,128,128]{3,2,1,0:T(8,128)(2,1)}, bf16[2,8,128,128]{3,2,1,0:T(8,128)(2,1)S(1)}, u32[]{:S(2)}, u32[]{:S(2)}) collective-permute-start(bf16[2,8,128,128]{3,2,1,0:T(8,128)(2,1)} %get-tuple-element.46), channel_id=1, source_target_pairs={{0,6},{2,4},{4,2},{6,0},{8,14},{10,12},{12,10},{14,8},{1,7},{3,5},... | collective-permute-start | bytes 1572872 | tf_op jit(solution)/shard_map/ppermute | solution.py:458
  187.5 17.6 %collective-permute-start.17 = (f32[8,128,128]{2,1,0:T(8,128)}, f32[8,128,128]{2,1,0:T(8,128)S(1)}, u32[]{:S(2)}, u32[]{:S(2)}) collective-permute-start(f32[8,128,128]{2,1,0:T(8,128)} %get-tuple-element.38), channel_id=1, source_target_pairs={{0,1},{1,0},{2,3},{3,2},{4,5},{5,4},{6,7},{7,6},{8,9},{9,8},{10,11... | collective-permute-start | bytes 1572872 | tf_op jit(solution)/shard_map/ppermute | solution.py:515
  187.6 12.0 %collective-permute-start.18 = (bf16[8,128,128]{2,1,0:T(8,128)(2,1)}, bf16[8,128,128]{2,1,0:T(8,128)(2,1)S(1)}, u32[]{:S(2)}, u32[]{:S(2)}) collective-permute-start(bf16[8,128,128]{2,1,0:T(8,128)(2,1)} %get-tuple-element.39), channel_id=1, source_target_pairs={{0,8},{1,9},{2,10},{3,11},{4,12},{5,13},{6,14},{7,15},{8,0},{9,1},... | collective-permute-start | bytes 786440 | tf_op jit(solution)/shard_map/ppermute | solution.py:454
  196.9 11.4 %collective-permute-start.23 = (f32[8,128,128]{2,1,0:T(8,128)}, f32[8,128,128]{2,1,0:T(8,128)S(1)}, u32[]{:S(2)}, u32[]{:S(2)}) collective-permute-start(f32[8,128,128]{2,1,0:T(8,128)} %get-tuple-element.48), channel_id=1, source_target_pairs={{0,1},{1,0},{2,3},{3,2},{4,5},{5,4},{6,7},{7,6},{8,9},{9,8},{10,11... | collective-permute-start | bytes 1572872 | tf_op jit(solution)/shard_map/ppermute | solution.py:517
  197.0 8.1 %collective-permute-start.19 = (bf16[8,128,128]{2,1,0:T(8,128)(2,1)S(1)}, bf16[8,128,128]{2,1,0:T(8,128)(2,1)S(1)}, u32[]{:S(2)}, u32[]{:S(2)}) collective-permute-start(bf16[8,128,128]{2,1,0:T(8,128)(2,1)S(1)} %copy-done.24), channel_id=1, source_target_pairs={{0,9},{1,8},{2,11},{3,10},{4,13},{5,12},{6,15},{7,14},{8,1},{9,0},... | collective-permute-start | bytes 786440 | tf_op jit(solution)/shard_map/ppermute | solution.py:454
  197.7 9.2 %collective-permute-start.24 = (bf16[8,128,128]{2,1,0:T(8,128)(2,1)}, bf16[8,128,128]{2,1,0:T(8,128)(2,1)S(1)}, u32[]{:S(2)}, u32[]{:S(2)}) collective-permute-start(bf16[8,128,128]{2,1,0:T(8,128)(2,1)} %get-tuple-element.49), channel_id=1, source_target_pairs={{0,6},{1,3},{2,4},{3,1},{4,2},{5,7},{6,0},{7,5},{8,14},{9,11},{10,... | collective-permute-start | bytes 786440 | tf_op jit(solution)/shard_map/ppermute | solution.py:454
  199.6 8.7 %collective-permute-start.25 = (bf16[8,128,128]{2,1,0:T(8,128)(2,1)}, bf16[8,128,128]{2,1,0:T(8,128)(2,1)S(1)}, u32[]{:S(2)}, u32[]{:S(2)}) collective-permute-start(bf16[8,128,128]{2,1,0:T(8,128)(2,1)} %get-tuple-element.50), channel_id=1, source_target_pairs={{0,3},{1,6},{2,1},{3,4},{4,7},{5,2},{6,5},{7,0},{8,11},{9,14},{10,... | collective-permute-start | bytes 786440 | tf_op jit(solution)/shard_map/ppermute | solution.py:454
  (20 other events, 81.8 us)
